TPU v7x, 768 devices: a whole 4x8x12 slice. The times are simulated.
768 devices in a mesh: lat: 48 (over y_lo, z), lon: 16 (over y_hi, x, core).
Axes of the slice: x: 4, y: 8 (y_hi: 2, y_lo: 4; y = y_hi * 4 + y_lo), z: 12, core: 2. Of those that a mesh axis runs over, the one named last changes fastest.
Arguments:
- state: float32 [5, 144, 8, 8, 2880], P(None, 'lat', None, None, 'lon'), may hold values from -6 to 6
- courant_x: float32 [144, 8, 8, 2880], P('lat', None, None, 'lon'), may hold values from -4 to 4
- courant_y: float32 [144, 8, 8, 2880], P('lat', None, None, 'lon'), may hold values from -4 to 4
- block_of_slot: int32 [144], P('lat'), may hold values from 0 to 143, as said below
- face_source: int32 [144, 2], P('lat'), may hold values from -1 to 143, as said below
- cutoff: int32 [1152], replicated, may hold values from 0 to 256, as said below
Outputs:
- new_state: float32 [5, 144, 8, 8, 2880], P(None, 'lat', None, None, 'lon')
Inputs may be any that keep to these rules, and one draw needn't show every extreme that they name: `block_of_slot`: each block number appears once. The polar blocks are the first and the last 24 block numbers; the 3 slots of one index of lat hold at most 2 polar blocks, and some index holds 2. `face_source`: entry 0 of slot s is the slot holding block block_of_slot[s] - 1 and entry 1 the slot holding block block_of_slot[s] + 1; -1 where that block does not exist. Rows of polar blocks have a cutoff of 1 or more; all other rows have 0.
All inputs are finite; a program needn't handle non-finite values.
Results may differ from a plain program's by a relative error of at most 0.00005.
Values sent between devices are 32-bit elements; how exact they have to be, the bound alone decides.
A program may use at most 64 MiB of HBM per device.

v0:
```python
import math

import jax
import jax.numpy as jnp
from jax import lax
from jax.sharding import PartitionSpec as P

NLON = 2880
KCUT = 256


def padded_2(array, sides, width):
    for axis, dim in sides:
        size, length = (lax.axis_size(axis), array.shape[dim])
        up = [(i, (i + 1) % size) for i in range(size)]
        down = [(j, i) for i, j in up]
        last = lax.slice_in_dim(array, length - width, length, axis=dim)
        leading = lax.slice_in_dim(array, 0, width, axis=dim)
        before = lax.ppermute(last, axis, up)
        after = lax.ppermute(leading, axis, down)
        array = jnp.concatenate([before, array, after], axis=dim)
    return array


def fourier_basis(columns):
    wavenumber = jnp.arange(KCUT, dtype=jnp.int32)
    phase = (columns[:, None] * wavenumber[None, :] % NLON).astype(jnp.float32) * (
        2.0 * math.pi / NLON
    )
    return jnp.concatenate([jnp.cos(phase), jnp.sin(phase)], axis=1)


def spectral_weights(cut_rows):
    wavenumber = jnp.arange(KCUT, dtype=jnp.int32)
    scaling = jnp.where(wavenumber == 0, 1.0 / NLON, 2.0 / NLON).astype(jnp.float32)
    kept = jnp.where(wavenumber[None, :] < cut_rows[:, None], scaling[None, :], 0.0)
    return jnp.concatenate([kept, kept], axis=1)


def shards(state, courant_x, courant_y, block_of_slot, face_source, cutoff):
    fields, slot_count, block_rows, levels, lon_width = state.shape
    first_rows, last_rows, last_wind = (
        lax.all_gather(state[:, :, 0], "lat", axis=1, tiled=True),
        lax.all_gather(state[:, :, block_rows - 1], "lat", axis=1, tiled=True),
        lax.all_gather(courant_y[:, block_rows - 1], "lat", axis=0, tiled=True),
    )
    north_slot = face_source[:, 0]
    south_slot = face_source[:, 1]
    has_north = north_slot >= 0
    has_south = south_slot >= 0
    north_safe = jnp.maximum(north_slot, 0)
    south_safe = jnp.maximum(south_slot, 0)
    north_rows = jnp.where(has_north[None, :, None, None], last_rows[:, north_safe], 0.0)
    south_rows = jnp.where(has_south[None, :, None, None], first_rows[:, south_safe], 0.0)
    north_wind = jnp.where(has_north[:, None, None], last_wind[north_safe], 0.0)
    extended = jnp.concatenate([north_rows[:, :, None], state, south_rows[:, :, None]], axis=2)
    wind_ext = jnp.concatenate([north_wind[:, None], courant_y], axis=1)
    face_keep = jnp.concatenate(
        [jnp.ones((slot_count, block_rows), jnp.float32), has_south[:, None].astype(jnp.float32)],
        axis=1,
    )
    merid_flux = (
        wind_ext[None]
        * (extended[:, :, :-1] + extended[:, :, 1:])
        * 0.5
        * face_keep[None, :, :, None, None]
    )
    merid_div = merid_flux[:, :, 1:] - merid_flux[:, :, :-1]
    stacked = jnp.concatenate([state, courant_x[None]], axis=0)
    padded = padded_2(stacked, (("lon", 4),), 1)
    field_ext = padded[:fields]
    zonal_wind = padded[fields]
    zonal_flux = zonal_wind[..., :-1] * (field_ext[..., :-1] + field_ext[..., 1:]) * 0.5
    zonal_div = zonal_flux[..., 1:] - zonal_flux[..., :-1]
    tendency = -(zonal_div + merid_div)
    global_rows = (
        block_of_slot[:, None] * block_rows + jnp.arange(block_rows, dtype=jnp.int32)[None, :]
    )
    latitudes = jnp.arange(cutoff.shape[0], dtype=jnp.int32)
    row_cut = jnp.sum(
        jnp.where(global_rows[:, :, None] == latitudes[None, None, :], cutoff[None, None, :], 0),
        axis=2,
    )
    chosen = tendency.shape[1]
    row_matrix = tendency.reshape(-1, lon_width)
    cut_rows = jnp.broadcast_to(
        row_cut[None, :, :, None], (fields, chosen, block_rows, levels)
    ).reshape(-1)
    columns_here = lax.axis_index("lon") * lon_width + jnp.arange(lon_width, dtype=jnp.int32)
    basis = fourier_basis(columns_here)
    partial_spec = jnp.dot(
        row_matrix, basis, precision=lax.Precision.HIGHEST, preferred_element_type=jnp.float32
    )
    spectrum = lax.psum(partial_spec, "lon")
    smoothed = jnp.dot(
        spectrum * spectral_weights(cut_rows),
        basis.T,
        precision=lax.Precision.HIGHEST,
        preferred_element_type=jnp.float32,
    )
    filtered = jnp.where(cut_rows[:, None] > 0, smoothed, row_matrix).reshape(tendency.shape)
    return state + filtered


def solution(mesh):
    placed = (
        P(None, "lat", None, None, "lon"),
        P("lat", None, None, "lon"),
        P("lat", None, None, "lon"),
        P("lat"),
        P("lat", None),
        P(),
    )
    return jax.shard_map(
        shards,
        mesh=mesh,
        in_specs=placed,
        out_specs=P(None, "lat", None, None, "lon"),
        check_vma=False,
    )
```

profile of v0, /device:TPU:1, one launch (start us, length us, event | category | flops | bytes accessed | tf_op | source)
XLA Modules:
  0.0 695.8 jit_solution(12912311710357235263)
XLA Ops:
  6.5 1.7 slice_bitcast_fusion
  8.2 0.0 all-gather.6.cloned.1.call-update
  8.2 0.0 all-gather.8.cloned.1.call-start
  8.3 0.7 all-gather.8.cloned.1.call-update
  9.0 0.0 all-reduce.3.cloned.1.call-start
  9.0 1.4 fusion.12
  10.5 0.0 copy-start.6
  10.5 0.0 slice-start
  10.5 0.9 copy.75
  11.4 4.6 collective-permute-start
  16.1 0.9 copy.76
  17.0 9.8 %collective-permute-start.1 = (f32[6,3,8,8,1]{3,2,4,1,0:T(8,128)S(1)}, f32[6,3,8,8,1]{3,2,4,1,0:T(8,128)}, u32[]{:S(2)}, u32[]{:S(2)}) collective-permute-start(f32[6,3,8,8,1]{3,2,4,1,0:T(8,128)S(1)} %copy.76), channel_id=1, source_target_pairs={{1,0},{2,1},{3,2},{4,3},{5,4},{6,5},{7,6},{8,7},{9,8},{10,9},{11,1... | collective-permute-start | bytes 13832 | tf_op jit(solution)/shard_map/ppermute | solution.py:20
  26.9 0.0 slice-done
  26.9 109.1 %all-gather = f32[144,1,8,180]{3,2,1,0:T(8,128)S(1)} all-gather(f32[3,1,8,180]{3,2,1,0:T(8,128)S(1)} %slice-done), channel_id=2, replica_groups=mesh['lat'=48,'lon'=16] {'lat'}, dimensions={0}, use_global_device_ids=true | all-gather | bytes 846720 | tf_op jit(solution)/shard_map/all_gather | solution.py:45
  135.9 0.5 gather_fusion
  136.5 0.6 slice_compare_fusion
  137.1 0.1 fusion.24
  137.2 0.7 pad_maximum_fusion.8
  137.9 1.6 fusion.20
  139.5 0.1 copy.72
  139.6 0.0 collective-permute-done
  139.6 0.9 copy.61
  140.5 0.0 collective-permute-done.1
  140.5 1.8 copy.62
  142.3 0.1 fusion.14
  142.4 0.5 fusion.10
  142.9 82.4 %all-gather.6.cloned.1.call-done = f32[5,144,1,8,180]{4,3,1,0,2:T(8,128)} async-done(((f32[5,3,1,8,180]{4,3,1,0,2:T(8,128)}), f32[5,144,1,8,180]{4,3,1,0,2:T(8,128)}) %all-gather.6.cloned.1.call-update) | async-done | bytes 4147216 | tf_op jit(solution)/shard_map/all_gather | solution.py:44
  225.3 3.2 gather_fusion.1
  228.5 228.3 %all-gather.8.cloned.1.call-done = f32[5,144,1,8,180]{4,3,1,0,2:T(8,128)} async-done(((f32[5,3,1,8,180]{4,3,1,0,2:T(8,128)}), f32[5,144,1,8,180]{4,3,1,0,2:T(8,128)}) %all-gather.8.cloned.1.call-update) | async-done | bytes 4147216 | tf_op jit(solution)/shard_map/all_gather | solution.py:43
  456.8 3.2 gather_fusion.2
  460.1 0.7 fusion.22
  460.8 1.1 fusion.5
  461.9 0.4 fusion.7
  462.3 0.5 copy-done.2
  462.8 0.1 copy-done.3
  462.9 3.0 fusion.13
  465.9 0.0 all-reduce.3.cloned.1.call-update
  465.9 0.6 copy-done.7
  466.6 0.1 iota_add_fusion
  466.6 0.2 select_reduce_fusion
  466.9 0.1 broadcast_in_dim.103
  466.9 0.1 broadcast_in_dim_reshape.4
  467.1 0.2 fusion.11
  467.3 1.2 copy.73
  468.4 213.7 %all-reduce.3.cloned.1.call-done = f32[960,512]{1,0:T(8,128)} async-done(((f32[960,512]{1,0:T(8,128)}), f32[960,512]{1,0:T(8,128)}) %all-reduce.3.cloned.1.call-update) | async-done | bytes 1966096 | tf_op jit(solution)/shard_map/psum | solution.py:94
  682.1 4.6 fusion.3
  686.7 1.4 copy.74
  688.2 1.1 add.59
  (21 shorter events, 0.1 us)
Async XLA Ops:
  6.5 218.8 %all-gather.6.cloned.1.call-start = ((), (), s32[]{:S(2)}) async-start(), calls=%async_computation.1 | async-start | bytes 6021120 | tf_op jit(solution)/shard_map/all_gather | solution.py:44
  8.2 448.6 %all-gather.8.cloned.1.call-start = ((), (), s32[]{:S(2)}) async-start(), calls=%async_computation.2 | async-start | bytes 6021120 | tf_op jit(solution)/shard_map/all_gather | solution.py:43
  9.0 673.1 %all-reduce.3.cloned.1.call-start = ((), (), s32[]{:S(2)}) async-start(), calls=%async_computation | async-start | bytes 3932160 | tf_op jit(solution)/shard_map/psum | solution.py:94
  10.5 16.3 %copy-start.6 = (s32[3,2]{0,1:T(2,128)S(1)}, s32[3,2]{0,1:T(2,128)}, u32[]{:S(2)}) copy-start(s32[3,2]{0,1:T(2,128)} %param.10) | copy-start | bytes 76
  10.5 16.4 %slice-start = ((f32[3,8,8,180]{3,2,1,0:T(8,128)}), f32[3,1,8,180]{3,2,1,0:T(8,128)S(1)}, s32[]{:S(2)}) async-start(f32[3,8,8,180]{3,2,1,0:T(8,128)} %param.8), calls=%async_computation.3 | async-start | bytes 49152 | tf_op jit(solution)/shard_map/slice | solution.py:45
  11.4 125.8 %copy-start.4 = (f32[3,8,8,180]{3,2,1,0:T(8,128)S(1)}, f32[3,8,8,180]{3,2,1,0:T(8,128)}, u32[]{:S(2)}) copy-start(f32[3,8,8,180]{3,2,1,0:T(8,128)} %param.8) | copy-start | bytes 414724
  11.4 128.2 %collective-permute-start = (f32[6,3,8,8,1]{3,2,4,1,0:T(8,128)S(1)}, f32[6,3,8,8,1]{3,2,4,1,0:T(8,128)S(1)}, u32[]{:S(2)}, u32[]{:S(2)}) collective-permute-start(f32[6,3,8,8,1]{3,2,4,1,0:T(8,128)S(1)} %copy.75), channel_id=1, source_target_pairs={{0,1},{1,2},{2,3},{3,4},{4,5},{5,6},{6,7},{7,8},{8,9},{9,10},{10,1... | collective-permute-start | bytes 13832 | tf_op jit(solution)/shard_map/ppermute | solution.py:19
  17.0 123.5 %collective-permute-start.1 = (f32[6,3,8,8,1]{3,2,4,1,0:T(8,128)S(1)}, f32[6,3,8,8,1]{3,2,4,1,0:T(8,128)}, u32[]{:S(2)}, u32[]{:S(2)}) collective-permute-start(f32[6,3,8,8,1]{3,2,4,1,0:T(8,128)S(1)} %copy.76), channel_id=1, source_target_pairs={{1,0},{2,1},{3,2},{4,3},{5,4},{6,5},{7,6},{8,7},{9,8},{10,9},{11,1... | collective-permute-start | bytes 13832 | tf_op jit(solution)/shard_map/ppermute | solution.py:20
  135.9 6.3 copy-start
  135.9 6.3 copy-start.1
  461.9 0.9 copy-start.2
  461.9 1.0 copy-start.3
  465.9 0.7 copy-start.7
  465.9 0.7 copy-start.5
Sparse Core Ops, SparseCore 0:
  9.7 215.4 all-gather.5
  227.7 229.0 all-gather.7
  466.1 216.0 all-reduce.2
where the time goes:
time: 696 us
  waiting for transfers between devices  525 us (75%)
  blocking collectives  109 us (16%)
  local copies, waits for them, and re-layouts  17.3 us (2%)
  starting transfers between devices  14.6 us (2%)
  between operations  13.3 us (2%)
  other arithmetic  8.8 us (1%)
  matrix products  7.57 us (1%)
    all_gather x1, waiting for transfers between devices, shards(): lax.all_gather(state[:, :, 0], 'lat', axis=1, tiled=True)  228 us
    psum x1, waiting for transfers between devices, shards(): spectrum = lax.psum(partial_spec, 'lon')  214 us
    all_gather x1, blocking collectives, shards(): lax.all_gather(courant_y[:, block_rows - 1], 'lat', axis=0, tiled=True)  109 us
    all_gather x1, waiting for transfers between devices, shards(): lax.all_gather(state[:, :, block_rows - 1], 'lat', axis=1, tiled=True)  82.4 us
  transfers between devices with their start and end apart: 5, of which 3 were waited for; matrix products, arithmetic and copies ran while one was open for 2% of the time, Pallas kernels for 0%

commit v1 on v0

v1 whole, which is shorter than its diff:
```python
import math

import jax
import jax.numpy as jnp
import numpy as np
from jax import lax
from jax.experimental import pallas as pl
from jax.experimental.pallas import tpu as pltpu
from jax.sharding import PartitionSpec as P

NLON = 2880
KCUT = 256
F, S, NR, L, W = 5, 3, 8, 8, 180
NBLK, POLAR = 144, 24
LANES = 256
NLAT, NLONDEV, HALF = 48, 16, 8
PIECES = NLAT * 8
MESH = pl.DeviceIdType.MESH
HIGHEST = lax.Precision.HIGHEST


def basis_table():
    column = np.arange(HALF * W, dtype=np.int64)
    phase = ((column[:, None] * np.arange(KCUT)[None, :]) % NLON) * (2.0 * math.pi / NLON)
    table = np.concatenate([np.cos(phase), np.sin(phase)], axis=1).reshape(HALF, W, 2 * KCUT)
    table = np.pad(table, ((0, 0), (0, LANES - W), (0, 0))).astype(np.float32)
    high = table.astype(jnp.bfloat16)
    low = (table - high.astype(np.float32)).astype(jnp.bfloat16)
    return np.stack([high, low])


def split2(x):
    high = x.astype(jnp.bfloat16)
    return high, (x - high.astype(jnp.float32)).astype(jnp.bfloat16)


def split3(x):
    high = x.astype(jnp.bfloat16)
    rest = x - high.astype(jnp.float32)
    mid = rest.astype(jnp.bfloat16)
    return high, mid, (rest - mid.astype(jnp.float32)).astype(jnp.bfloat16)


def dot(a, b, dims):
    return lax.dot_general(a, b, (dims, ((), ())), preferred_element_type=jnp.float32)


def store_rows(ref, c, t, value):
    for part in range(2):
        ref[pl.ds(c * 128 + part * 8 + t, L, stride=16), :] = value[:, part * 128:(part + 1) * 128]


def load_rows(ref, c, t):
    return jnp.concatenate([ref[pl.ds(c * 128 + part * 8 + t, L, stride=16), :] for part in range(2)], axis=1)


def iota(shape, dim):
    return lax.broadcasted_iota(jnp.int32, shape, dim)


def step_kernel(
    block_ref, face_ref, cut_ref, state_ref, cx_ref, cy_ref, table_hbm,
    out_ref,
    table, padded, send1, got1, send2, halo,
    edges, from_west, from_east, east_in, west_in,
    tend, rows_out, rows_in, spec, spec_in, smooth_out, smooth_in,
    table_sem, s1, r1, s2, r2, edge_send, edge_recv, a_send, a_recv, y_send, y_recv, b_send, b_recv,
):
    lat, lon = lax.axis_index("lat"), lax.axis_index("lon")
    half, seat = lon // HALF, lon % HALF
    partner = (lon + HALF) % NLONDEV
    east, west = (lon + 1) % NLONDEV, (lon + NLONDEV - 1) % NLONDEV

    load_table = pltpu.make_async_copy(table_hbm, table, table_sem)
    load_table.start()

    barrier = pltpu.get_barrier_semaphore()

    @pl.loop(1, NLAT)
    def _(i):
        pl.semaphore_signal(barrier, inc=1, device_id={"lat": (lat + i) % NLAT}, device_id_type=MESH)

    @pl.loop(1, NLONDEV)
    def _(i):
        pl.semaphore_signal(barrier, inc=1, device_id={"lon": (lon + i) % NLONDEV}, device_id_type=MESH)

    blocks = [block_ref[s] for s in range(S)]
    polar = [jnp.where(b < POLAR, 1, 0) + jnp.where(b >= NBLK - POLAR, 1, 0) for b in blocks]
    cols, keep = [], []
    for t in range(2 * S):
        n = face_ref[t % S, t // S]
        safe = jnp.maximum(n, 0)
        cols.append(jnp.where(n >= 0, 8 * lax.div(safe, S) + lax.rem(safe, S) + (t // S) * S, -1))
        keep.append(jnp.where(n >= 0, 1.0, 0.0))
    keep = keep[S:]
    first = (1 - polar[0]) * polar[2]
    picks = [first, 1 + polar[2]]

    lane = iota((L, LANES), 1)

    send1[...] = jnp.zeros_like(send1)
    padded[...] = jnp.zeros_like(padded)
    padded[:, :W] = state_ref[...].reshape(F * S * NR * L, W)

    def tile(f, s, r):
        return padded[pl.ds(pl.multiple_of(((f * S + s) * NR + r) * L, L), L), :]

    for t in range(2 * S):
        s = t % S
        want = jnp.full((L, LANES), cols[t].astype(jnp.float32), jnp.float32)
        for f in range(F):
            row = tile(f, s, NR - 1 if t < S else 0)
            store_rows(send1, f, t, jnp.where(lane == W, want, row))
        if t < S:
            wind = jnp.concatenate([cy_ref[s, NR - 1], jnp.zeros((L, LANES - W), jnp.float32)], axis=1)
            store_rows(send1, F, t, jnp.where(lane == W, want, wind))
        else:
            store_rows(send1, F, t, jnp.where(lane == W, want, 0.0))

    pick = jnp.where(
        jnp.logical_or(
            jnp.logical_and(iota((8, W), 0) == 0, iota((8, W), 1) == 0),
            jnp.logical_and(iota((8, W), 0) == 1, iota((8, W), 1) == W - 1),
        ),
        1.0, 0.0,
    ).astype(jnp.float32)
    edges[...] = jnp.zeros_like(edges)
    edges[:, :960] = lax.dot_general(
        pick, state_ref[...].reshape(F * S * NR * L, W), (((1,), (1,)), ((), ())),
        precision=HIGHEST, preferred_element_type=jnp.float32)
    edges[:, 1024:1216] = lax.dot_general(
        pick, cx_ref[...].reshape(S * NR * L, W), (((1,), (1,)), ((), ())),
        precision=HIGHEST, preferred_element_type=jnp.float32)

    pl.semaphore_wait(barrier, NLAT - 1 + NLONDEV - 1)

    def piece(ref, i):
        return ref.at[pl.ds(pl.multiple_of(i * 16, 16), 16), :]

    @pl.loop(1, NLAT)
    def _(i):
        to = (lat + i) % NLAT
        pltpu.make_async_remote_copy(
            piece(send1, to), piece(got1, lat), s1, r1, device_id={"lat": to}, device_id_type=MESH).start()

    to_west = pltpu.make_async_remote_copy(
        edges, from_east, edge_send.at[0], edge_recv.at[0], device_id={"lon": west}, device_id_type=MESH)
    to_east = pltpu.make_async_remote_copy(
        edges, from_west, edge_send.at[1], edge_recv.at[1], device_id={"lon": east}, device_id_type=MESH)
    to_west.start()
    to_east.start()
    mine = pl.ds(pl.multiple_of(lat * 16, 16), 16)
    got1[mine, :] = send1[mine, :]

    def wait_pieces(sem, ref):
        whole = ref.at[pl.ds(0, 16 * (NLAT - 1)), :]
        pltpu.make_async_copy(whole, whole, sem).wait()

    wait_pieces(r1, got1)
    parts = got1[...].reshape(NLAT, 2, 8, 128)
    pieces = jnp.concatenate([parts[:, i].reshape(PIECES, 128) for i in range(2)], axis=1)
    asked = jnp.broadcast_to(pieces[:, W:W + 1], (PIECES, PIECES))
    onehot = jnp.where(asked == iota((PIECES, PIECES), 1).astype(jnp.float32), 1.0, 0.0).astype(jnp.bfloat16)
    a, b, c = split3(pieces)
    nn = ((1,), (0,))
    found = (dot(onehot, a, nn) + dot(onehot, b, nn)) + dot(onehot, c, nn)
    send2[...] = jnp.stack(
        [found[:, i * 128:(i + 1) * 128].reshape(NLAT, 8, 128) for i in range(2)], axis=1).reshape(2 * PIECES, 128)

    @pl.loop(1, NLAT)
    def _(i):
        to = (lat + i) % NLAT
        pltpu.make_async_remote_copy(
            piece(send2, to), piece(halo, lat), s2, r2, device_id={"lat": to}, device_id_type=MESH).start()

    halo[mine, :] = send2[mine, :]

    to_west.wait()
    to_east.wait()
    place = lambda src, dst: jnp.where(
        jnp.logical_and(iota((8, LANES), 0) == src, iota((8, LANES), 1) == dst), 1.0, 0.0).astype(jnp.float32)
    tn = (((0,), (0,)), ((), ()))
    east_in[...] = lax.dot_general(
        from_east[...], place(0, W - 1), tn, precision=HIGHEST, preferred_element_type=jnp.float32)
    west_in[...] = lax.dot_general(
        from_west[...], place(1, 0), tn, precision=HIGHEST, preferred_element_type=jnp.float32)
    wait_pieces(r2, halo)

    zeros = jnp.zeros((L, LANES - W), jnp.float32)

    for s in range(S):
        kept = jnp.full((L, LANES), keep[s], jnp.float32)

        @pl.loop(0, F)
        def _(f):
            above, below = load_rows(halo, f, s), load_rows(halo, f, S + s)
            north_wind = load_rows(halo, F, s)
            here = tile(f, s, 0)
            flux = north_wind * (above + here) * 0.5
            for r in range(NR):
                at = pl.ds(pl.multiple_of(((f * S + s) * NR + r) * L, L), L)
                wind = jnp.concatenate([cy_ref[s, r], zeros], axis=1)
                zonal = jnp.concatenate([cx_ref[s, r], zeros], axis=1)
                after = tile(f, s, r + 1) if r < NR - 1 else below
                next_flux = wind * (here + after) * 0.5
                if r == NR - 1:
                    next_flux = next_flux * kept
                to_the_east = jnp.where(lane == W - 1, east_in[at, :], pltpu.roll(here, LANES - 1, 1))
                across = zonal * (here + to_the_east) * 0.5
                cw = west_in[pl.ds(1024 + (s * NR + r) * L, L), :]
                from_the_west = jnp.where(
                    lane == 0, cw * (west_in[at, :] + here) * 0.5, pltpu.roll(across, 1, 1))
                value = -((across - from_the_west) + (next_flux - flux))
                tend[pl.ds(pl.multiple_of(((s * F + f) * NR + r) * L, L), L), :] = jnp.where(lane < W, value, 0.0)
                flux, here = next_flux, after

    for k in range(2):
        upper = jnp.full((L, LANES), picks[k], jnp.int32) == k + 1

        @pl.loop(0, F)
        def _(f):
            for r in range(NR):
                low, high = [
                    tend[pl.ds(pl.multiple_of(((s * F + f) * NR + r) * L, L), L), :] for s in (k, k + 1)]
                rows_out[r, k, pl.ds(pl.multiple_of(f * L, L), L), :] = jnp.where(upper, high, low)

    def out_copy(k, i):
        to = (seat + i) % HALF
        return pltpu.make_async_remote_copy(
            rows_out.at[to, k], rows_in.at[seat, k], a_send.at[k, to], a_recv.at[k, seat],
            device_id={"lon": half * HALF + to}, device_id_type=MESH)

    def in_wait(k, i):
        source = (seat + HALF - i) % HALF
        pltpu.make_async_remote_copy(
            rows_out.at[source, k], rows_in.at[source, k], a_send.at[k, source], a_recv.at[k, source],
            device_id={"lon": half * HALF + source}, device_id_type=MESH).wait_recv()

    for k in range(2):
        for i in range(1, HALF):
            out_copy(k, i).start()
    rows_in[seat] = rows_out[seat]
    load_table.wait()

    def forward(k):
        for i in range(1, HALF):
            in_wait(k, i)
        total = jnp.zeros((F * L, 2 * KCUT), jnp.float32)
        for d in range(HALF):
            xh, xl = split2(rows_in[d, k])
            total += dot(xh, table[0, d], nn) + (dot(xl, table[0, d], nn) + dot(xh, table[1, d], nn))
        spec[k] = total

    def swap(k):
        return pltpu.make_async_remote_copy(
            spec.at[k], spec_in.at[k], y_send.at[k], y_recv.at[k], device_id={"lon": partner}, device_id_type=MESH)

    for k in range(2):
        forward(k)
        swap(k).start()

    wave = iota((F * L, 2 * KCUT), 1) % KCUT
    sign = jnp.where(wave % 2 == 0, 1.0, -1.0)
    scale = jnp.where(wave == 0, 1.0 / NLON, 2.0 / NLON)
    nt = ((1,), (1,))

    def back_copy(k, i):
        to = (seat + i) % HALF
        return pltpu.make_async_remote_copy(
            smooth_out.at[to, k], smooth_in.at[seat, k], b_send.at[k, to], b_recv.at[k, seat],
            device_id={"lon": half * HALF + to}, device_id_type=MESH)

    def back_wait(k, i):
        source = (seat + HALF - i) % HALF
        pltpu.make_async_remote_copy(
            smooth_out.at[source, k], smooth_in.at[source, k], b_send.at[k, source], b_recv.at[k, source],
            device_id={"lon": half * HALF + source}, device_id_type=MESH).wait_recv()

    for k in range(2):
        swap(k).wait()
        block = jnp.where(picks[k] == k + 1, blocks[k + 1], blocks[k])
        limit = cut_ref[block * NR + seat]
        kept = jnp.where(wave < jnp.full(wave.shape, limit, jnp.int32), scale, 0.0)
        xh, xl = split2((spec[k] + sign * spec_in[k]) * kept)
        for d in range(HALF):
            smooth_out[d, k] = dot(xh, table[0, d], nt) + (dot(xl, table[0, d], nt) + dot(xh, table[1, d], nt))
        for i in range(1, HALF):
            back_copy(k, i).start()
        smooth_in[seat, k] = smooth_out[seat, k]

    for k in range(2):
        for i in range(1, HALF):
            back_wait(k, i)

    for s in range(S):
        use = [
            jnp.full((L, LANES), jnp.where(picks[k] == s, polar[s], 0), jnp.int32) > 0
            for k in range(2)
        ]

        @pl.loop(0, F)
        def _(f):
            for r in range(NR):
                value = tend[pl.ds(pl.multiple_of(((s * F + f) * NR + r) * L, L), L), :]
                for k in range(2):
                    value = jnp.where(use[k], smooth_in[r, k, pl.ds(pl.multiple_of(f * L, L), L), :], value)
                out_ref[f, s, r] = value[:, :W]

    wait_pieces(s1, send1)
    wait_pieces(s2, send2)
    for k in range(2):
        for i in range(1, HALF):
            out_copy(k, i).wait_send()
            back_copy(k, i).wait_send()


def shards(table, state, courant_x, courant_y, block_of_slot, face_source, cutoff):
    vmem = pl.BlockSpec(memory_space=pltpu.VMEM)
    smem = pl.BlockSpec(memory_space=pltpu.SMEM)
    f32 = jnp.float32
    rows = F * S * NR * L
    dma = pltpu.SemaphoreType.DMA
    filtered = pl.pallas_call(
        step_kernel,
        out_shape=jax.ShapeDtypeStruct((F, S, NR, L, W), f32),
        in_specs=[smem, smem, smem, vmem, vmem, vmem, pl.BlockSpec(memory_space=pl.ANY)],
        out_specs=vmem,
        scratch_shapes=[
            pltpu.VMEM((2, HALF, LANES, 2 * KCUT), jnp.bfloat16),
            pltpu.VMEM((rows, LANES), f32),
            pltpu.VMEM((2 * PIECES, 128), f32),
            pltpu.VMEM((2 * PIECES, 128), f32),
            pltpu.VMEM((2 * PIECES, 128), f32),
            pltpu.VMEM((2 * PIECES, 128), f32),
            pltpu.VMEM((8, 1280), f32),
            pltpu.VMEM((8, 1280), f32),
            pltpu.VMEM((8, 1280), f32),
            pltpu.VMEM((1280, LANES), f32),
            pltpu.VMEM((1280, LANES), f32),
            pltpu.VMEM((rows, LANES), f32),
            pltpu.VMEM((NR, 2, F * L, LANES), f32),
            pltpu.VMEM((NR, 2, F * L, LANES), f32),
            pltpu.VMEM((2, F * L, 2 * KCUT), f32),
            pltpu.VMEM((2, F * L, 2 * KCUT), f32),
            pltpu.VMEM((NR, 2, F * L, LANES), f32),
            pltpu.VMEM((NR, 2, F * L, LANES), f32),
            dma, dma, dma, dma, dma,
            dma((2,)), dma((2,)),
            dma((2, HALF)), dma((2, HALF)),
            dma((2,)), dma((2,)),
            dma((2, HALF)), dma((2, HALF)),
        ],
        compiler_params=pltpu.CompilerParams(
            collective_id=0, has_side_effects=True, vmem_limit_bytes=48 << 20),
    )(block_of_slot, face_source, cutoff, state, courant_x, courant_y, table)
    return state + filtered


def solution(mesh):
    placed = (
        P(),
        P(None, "lat", None, None, "lon"),
        P("lat", None, None, "lon"),
        P("lat", None, None, "lon"),
        P("lat"),
        P("lat", None),
        P(),
    )
    body = jax.shard_map(
        shards,
        mesh=mesh,
        in_specs=placed,
        out_specs=P(None, "lat", None, None, "lon"),
        check_vma=False,
    )
    table = basis_table()
    return lambda *arrays: body(jnp.asarray(table), *arrays)
```

time: 696 us -> 90.9 us (0.13)
  waiting for transfers between devices: 525 us -> 0 us
  blocking collectives: 109 us -> 0 us
  Pallas kernels: 0 us -> 83.8 us
  starting transfers between devices: 14.6 us -> 0 us
  between operations: 13.3 us -> 0.01 us
  local copies, waits for them, and re-layouts: 17.3 us -> 5.17 us
  other arithmetic: 8.8 us -> 1.09 us
  matrix products: 7.57 us -> 0 us
    all_gather x2 -> x0, waiting for transfers between devices: 311 us -> none  [the longest x1 228 us: shards(): lax.all_gather(state[:, :, 0], 'lat', axis=1, tiled=True)]
    psum x1 -> x0, waiting for transfers between devices: 214 us -> none  [shards(): spectrum = lax.psum(partial_spec, 'lon')]
    all_gather x1 -> x0, blocking collectives: 109 us -> none  [shards(): lax.all_gather(courant_y[:, block_rows - 1], 'lat', axis=0, tiled=True)]
    pallas_call x0 -> x1, Pallas kernels: none -> 83.8 us  [shards(): pl.pallas_call(step_kernel, out_shape=jax.ShapeDtypeStruct((F, S, NR, L,...]
    ppermute x2 -> x0, starting transfers between devices: 14.5 us -> none  [the longest x1 9.84 us: padded_2(): after = lax.ppermute(leading, axis, down)]
    dot_general x2 -> x0, matrix products: 7.57 us -> none  [the longest x1 4.61 us: shards(): jnp.dot(spectrum * spectral_weights(cut_rows), basis.T, precision=lax.Pre...]
    gather x3 -> x0, local copies, waits for them, and re-layouts: 7 us -> none  [the longest x1 3.22 us: shards(): last_rows[:, north_safe]]
  transfers between devices with their start and end apart: 5 -> 0, of which waited for: 3 -> 0; matrix products, arithmetic and copies ran while one was open for 2% -> 0% of each run, Pallas kernels for 0% -> 0%
where the time goes in v1:
time: 90.9 us; the launch traced here: 90.1 us
  Pallas kernels  83.8 us (92%)
  local copies, waits for them, and re-layouts  5.17 us (6%)
  other arithmetic  1.09 us (1%)
    pallas_call x1, Pallas kernels, shards(): pl.pallas_call(step_kernel, out_shape=jax.ShapeDtypeStruct((F, S, NR, L,...  83.8 us
    unnamed x11, local copies, waits for them, and re-layouts  5.17 us

profile of v1, /device:TPU:1, one launch (start us, length us, event | category | flops | bytes accessed | tf_op | source)
XLA Modules:
  0.0 90.1 jit_solution(9988318457850408835)
XLA Ops:
  0.0 0.8 copy.8.face_ref
  0.8 0.0 copy-start
  0.8 1.2 %copy-done = f32[5,3,8,8,180]{4,3,2,1,0:T(8,128)S(1)} copy-done((f32[5,3,8,8,180]{4,3,2,1,0:T(8,128)S(1)}, f32[5,3,8,8,180]{4,3,2,1,0:T(8,128)}, u32[]{:S(2)}) %copy-start) | copy-done | bytes 691224
  2.0 0.0 copy-start.1
  2.0 0.9 %copy-done.1 = f32[3,8,8,180]{3,2,1,0:T(8,128)S(1)} copy-done((f32[3,8,8,180]{3,2,1,0:T(8,128)S(1)}, f32[3,8,8,180]{3,2,1,0:T(8,128)}, u32[]{:S(2)}) %copy-start.1) | copy-done | bytes 138264
  2.9 0.0 copy-start.2
  2.9 0.9 %copy-done.2 = f32[3,8,8,180]{3,2,1,0:T(8,128)S(1)} copy-done((f32[3,8,8,180]{3,2,1,0:T(8,128)S(1)}, f32[3,8,8,180]{3,2,1,0:T(8,128)}, u32[]{:S(2)}) %copy-start.2) | copy-done | bytes 138264
  3.8 0.0 copy-start.3
  3.8 0.7 copy-done.3
  4.5 0.0 copy-start.4
  4.5 0.7 copy-done.4
  5.2 83.8 %shard_map.73 = f32[5,3,8,8,180]{4,3,2,1,0:T(8,128)S(1)} custom-call(s32[3]{0:T(128)S(1)} %copy-done.4, s32[3,2]{1,0:T(4,128)S(1)} %copy.8.face_ref, s32[1152]{0:T(1024)S(1)} %copy-done.3, f32[5,3,8,8,180]{4,3,2,1,0:T(8,128)S(1)} %copy-done, f32[3,8,8,180]{3,2,1,0:T(8,128)S(1)} %copy-done.1, f32[3,8,8,180]{3,2,1,0:T(8,128)S(1)} %copy-done.2, ...), custom_call_target="tpu_custom_call" | custom-call | tf_op jit(solution)/shard_map/pallas_call | solution.py:323
  89.0 1.1 %add.3 = f32[5,3,8,8,180]{4,3,2,1,0:T(8,128)} add(f32[5,3,8,8,180]{4,3,2,1,0:T(8,128)S(1)} %copy-done, f32[5,3,8,8,180]{4,3,2,1,0:T(8,128)S(1)} %shard_map.73) | non-fusion elementwise | flops 172800 | bytes 2073600 | tf_op jit(solution)/shard_map/add | solution.py:356
Async XLA Ops:
  0.8 1.2 %copy-start = (f32[5,3,8,8,180]{4,3,2,1,0:T(8,128)S(1)}, f32[5,3,8,8,180]{4,3,2,1,0:T(8,128)}, u32[]{:S(2)}) copy-start(f32[5,3,8,8,180]{4,3,2,1,0:T(8,128)} %state_ref.1) | copy-start | bytes 2073604
  2.0 0.9 %copy-start.1 = (f32[3,8,8,180]{3,2,1,0:T(8,128)S(1)}, f32[3,8,8,180]{3,2,1,0:T(8,128)}, u32[]{:S(2)}) copy-start(f32[3,8,8,180]{3,2,1,0:T(8,128)} %cx_ref.1) | copy-start | bytes 414724
  2.9 0.9 %copy-start.2 = (f32[3,8,8,180]{3,2,1,0:T(8,128)S(1)}, f32[3,8,8,180]{3,2,1,0:T(8,128)}, u32[]{:S(2)}) copy-start(f32[3,8,8,180]{3,2,1,0:T(8,128)} %cy_ref.1) | copy-start | bytes 414724
  3.8 0.7 copy-start.3
  4.5 0.7 copy-start.4

commit v2 on v1

--- a/solution.py
+++ b/solution.py
@@ -45,13 +45,35 @@
     return lax.dot_general(a, b, (dims, ((), ())), preferred_element_type=jnp.float32)
 
 
-def store_rows(ref, c, t, value):
-    for part in range(2):
-        ref[pl.ds(c * 128 + part * 8 + t, L, stride=16), :] = value[:, part * 128:(part + 1) * 128]
-
-
-def load_rows(ref, c, t):
-    return jnp.concatenate([ref[pl.ds(c * 128 + part * 8 + t, L, stride=16), :] for part in range(2)], axis=1)
+def store_rows(main, tail, c, t, value):
+    main[pl.ds(c * 64 + t, L, stride=8), :] = value[:, :128]
+    tail[pl.ds(c * 64 + t, L, stride=8), :] = value[:, 128:]
+
+
+def load_rows(main, tail, c, t):
+    at = pl.ds(c * 64 + t, L, stride=8)
+    return jnp.concatenate([main[at, :], tail[at, :]], axis=1)
+
+
+def pack(main, tail):
+    shape = (NLAT, 8, 128)
+    main, tail = main.reshape(shape), tail.reshape(shape)
+    sub, lane = iota(shape, 1), iota(shape, 2)
+    pairs = jnp.where(lane < 64, tail, pltpu.roll(pltpu.roll(tail, 5, 1), 64, 2))
+    first = jnp.where(sub < 6, main, pltpu.roll(pairs, 6, 1))
+    return jnp.stack([first, pltpu.roll(pairs, 6, 1)], axis=1).reshape(2 * PIECES, 128)
+
+
+def unpack(packed):
+    shape = (NLAT, 8, 128)
+    sub = iota(shape, 1)
+    packed = packed.reshape(NLAT, 2, 8, 128)
+    first, second = packed[:, 0], packed[:, 1]
+    pairs = jnp.where(sub < 2, pltpu.roll(first, 2, 1), pltpu.roll(second, 2, 1))
+    tail = jnp.where(sub < 3, pairs, pltpu.roll(pltpu.roll(pairs, 3, 1), 64, 2))
+    keep = sub < 6
+    main, tail = jnp.where(keep, first, 0.0), jnp.where(keep, tail, 0.0)
+    return main.reshape(PIECES, 128), tail.reshape(PIECES, 128)
 
 
 def iota(shape, dim):
@@ -59,36 +81,41 @@
 
 
 def step_kernel(
-    block_ref, face_ref, cut_ref, state_ref, cx_ref, cy_ref, table_hbm,
+    block_in, face_in, cut_in, state_in, cx_in, cy_in, table_hbm,
     out_ref,
-    table, padded, send1, got1, send2, halo,
+    block_ref, face_ref, cut_ref, state_ref, cx_ref, cy_ref,
+    table, padded, main, tail, send1, got1, send2, halo,
     edges, from_west, from_east, east_in, west_in,
     tend, rows_out, rows_in, spec, spec_in, smooth_out, smooth_in,
-    table_sem, s1, r1, s2, r2, edge_send, edge_recv, a_send, a_recv, y_send, y_recv, b_send, b_recv,
+    load_sem, table_sem, s1, r1, s2, r2, edge_send, edge_recv, a_send, a_recv, y_send, y_recv, b_send, b_recv,
 ):
     lat, lon = lax.axis_index("lat"), lax.axis_index("lon")
     half, seat = lon // HALF, lon % HALF
     partner = (lon + HALF) % NLONDEV
     east, west = (lon + 1) % NLONDEV, (lon + NLONDEV - 1) % NLONDEV
 
+    loads = [
+        pltpu.make_async_copy(source, target, load_sem.at[i])
+        for i, (source, target) in enumerate([
+            (state_in, state_ref), (cy_in, cy_ref), (face_in, face_ref),
+            (block_in, block_ref), (cx_in, cx_ref), (cut_in, cut_ref)])
+    ]
+    for load in loads:
+        load.start()
     load_table = pltpu.make_async_copy(table_hbm, table, table_sem)
     load_table.start()
-
-    barrier = pltpu.get_barrier_semaphore()
-
-    @pl.loop(1, NLAT)
-    def _(i):
-        pl.semaphore_signal(barrier, inc=1, device_id={"lat": (lat + i) % NLAT}, device_id_type=MESH)
-
-    @pl.loop(1, NLONDEV)
-    def _(i):
-        pl.semaphore_signal(barrier, inc=1, device_id={"lon": (lon + i) % NLONDEV}, device_id_type=MESH)
+    main[...] = jnp.zeros_like(main)
+    tail[...] = jnp.zeros_like(tail)
+    padded[...] = jnp.zeros_like(padded)
+    edges[...] = jnp.zeros_like(edges)
+    for load in loads:
+        load.wait()
 
     blocks = [block_ref[s] for s in range(S)]
     polar = [jnp.where(b < POLAR, 1, 0) + jnp.where(b >= NBLK - POLAR, 1, 0) for b in blocks]
     cols, keep = [], []
     for t in range(2 * S):
-        n = face_ref[t % S, t // S]
+        n = face_ref[t // S, t % S]
         safe = jnp.maximum(n, 0)
         cols.append(jnp.where(n >= 0, 8 * lax.div(safe, S) + lax.rem(safe, S) + (t // S) * S, -1))
         keep.append(jnp.where(n >= 0, 1.0, 0.0))
@@ -98,8 +125,6 @@
 
     lane = iota((L, LANES), 1)
 
-    send1[...] = jnp.zeros_like(send1)
-    padded[...] = jnp.zeros_like(padded)
     padded[:, :W] = state_ref[...].reshape(F * S * NR * L, W)
 
     def tile(f, s, r):
@@ -110,12 +135,14 @@
         want = jnp.full((L, LANES), cols[t].astype(jnp.float32), jnp.float32)
         for f in range(F):
             row = tile(f, s, NR - 1 if t < S else 0)
-            store_rows(send1, f, t, jnp.where(lane == W, want, row))
+            store_rows(main, tail, f, t, jnp.where(lane == W, want, row))
         if t < S:
             wind = jnp.concatenate([cy_ref[s, NR - 1], jnp.zeros((L, LANES - W), jnp.float32)], axis=1)
-            store_rows(send1, F, t, jnp.where(lane == W, want, wind))
+            store_rows(main, tail, F, t, jnp.where(lane == W, want, wind))
         else:
-            store_rows(send1, F, t, jnp.where(lane == W, want, 0.0))
+            store_rows(main, tail, F, t, jnp.where(lane == W, want, 0.0))
+
+    send1[...] = pack(main[...], tail[...])
 
     pick = jnp.where(
         jnp.logical_or(
@@ -124,7 +151,6 @@
         ),
         1.0, 0.0,
     ).astype(jnp.float32)
-    edges[...] = jnp.zeros_like(edges)
     edges[:, :960] = lax.dot_general(
         pick, state_ref[...].reshape(F * S * NR * L, W), (((1,), (1,)), ((), ())),
         precision=HIGHEST, preferred_element_type=jnp.float32)
@@ -132,10 +158,8 @@
         pick, cx_ref[...].reshape(S * NR * L, W), (((1,), (1,)), ((), ())),
         precision=HIGHEST, preferred_element_type=jnp.float32)
 
-    pl.semaphore_wait(barrier, NLAT - 1 + NLONDEV - 1)
-
     def piece(ref, i):
-        return ref.at[pl.ds(pl.multiple_of(i * 16, 16), 16), :]
+        return ref.at[pl.ds(pl.multiple_of(i * 16, 16), 9), :]
 
     @pl.loop(1, NLAT)
     def _(i):
@@ -153,19 +177,17 @@
     got1[mine, :] = send1[mine, :]
 
     def wait_pieces(sem, ref):
-        whole = ref.at[pl.ds(0, 16 * (NLAT - 1)), :]
+        whole = ref.at[pl.ds(0, 9 * (NLAT - 1)), :]
         pltpu.make_async_copy(whole, whole, sem).wait()
 
     wait_pieces(r1, got1)
-    parts = got1[...].reshape(NLAT, 2, 8, 128)
-    pieces = jnp.concatenate([parts[:, i].reshape(PIECES, 128) for i in range(2)], axis=1)
+    pieces = jnp.concatenate(unpack(got1[...]), axis=1)
     asked = jnp.broadcast_to(pieces[:, W:W + 1], (PIECES, PIECES))
     onehot = jnp.where(asked == iota((PIECES, PIECES), 1).astype(jnp.float32), 1.0, 0.0).astype(jnp.bfloat16)
     a, b, c = split3(pieces)
     nn = ((1,), (0,))
     found = (dot(onehot, a, nn) + dot(onehot, b, nn)) + dot(onehot, c, nn)
-    send2[...] = jnp.stack(
-        [found[:, i * 128:(i + 1) * 128].reshape(NLAT, 8, 128) for i in range(2)], axis=1).reshape(2 * PIECES, 128)
+    send2[...] = pack(found[:, :128], found[:, 128:])
 
     @pl.loop(1, NLAT)
     def _(i):
@@ -185,6 +207,7 @@
     west_in[...] = lax.dot_general(
         from_west[...], place(1, 0), tn, precision=HIGHEST, preferred_element_type=jnp.float32)
     wait_pieces(r2, halo)
+    main[...], tail[...] = unpack(halo[...])
 
     zeros = jnp.zeros((L, LANES - W), jnp.float32)
 
@@ -193,8 +216,8 @@
 
         @pl.loop(0, F)
         def _(f):
-            above, below = load_rows(halo, f, s), load_rows(halo, f, S + s)
-            north_wind = load_rows(halo, F, s)
+            above, below = load_rows(main, tail, f, s), load_rows(main, tail, f, S + s)
+            north_wind = load_rows(main, tail, F, s)
             here = tile(f, s, 0)
             flux = north_wind * (above + here) * 0.5
             for r in range(NR):
@@ -316,18 +339,26 @@
 
 def shards(table, state, courant_x, courant_y, block_of_slot, face_source, cutoff):
     vmem = pl.BlockSpec(memory_space=pltpu.VMEM)
-    smem = pl.BlockSpec(memory_space=pltpu.SMEM)
+    i32 = jnp.int32
     f32 = jnp.float32
     rows = F * S * NR * L
     dma = pltpu.SemaphoreType.DMA
     filtered = pl.pallas_call(
         step_kernel,
         out_shape=jax.ShapeDtypeStruct((F, S, NR, L, W), f32),
-        in_specs=[smem, smem, smem, vmem, vmem, vmem, pl.BlockSpec(memory_space=pl.ANY)],
+        in_specs=[pl.BlockSpec(memory_space=pltpu.HBM)] * 7,
         out_specs=vmem,
         scratch_shapes=[
+            pltpu.SMEM((S,), i32),
+            pltpu.SMEM((2, S), i32),
+            pltpu.SMEM((NBLK * NR,), i32),
+            pltpu.VMEM((F, S, NR, L, W), f32),
+            pltpu.VMEM((S, NR, L, W), f32),
+            pltpu.VMEM((S, NR, L, W), f32),
             pltpu.VMEM((2, HALF, LANES, 2 * KCUT), jnp.bfloat16),
             pltpu.VMEM((rows, LANES), f32),
+            pltpu.VMEM((PIECES, 128), f32),
+            pltpu.VMEM((PIECES, 128), f32),
             pltpu.VMEM((2 * PIECES, 128), f32),
             pltpu.VMEM((2 * PIECES, 128), f32),
             pltpu.VMEM((2 * PIECES, 128), f32),
@@ -344,15 +375,15 @@
             pltpu.VMEM((2, F * L, 2 * KCUT), f32),
             pltpu.VMEM((NR, 2, F * L, LANES), f32),
             pltpu.VMEM((NR, 2, F * L, LANES), f32),
-            dma, dma, dma, dma, dma,
+            dma((6,)), dma, dma, dma, dma, dma,
             dma((2,)), dma((2,)),
             dma((2, HALF)), dma((2, HALF)),
             dma((2,)), dma((2,)),
             dma((2, HALF)), dma((2, HALF)),
         ],
         compiler_params=pltpu.CompilerParams(
-            collective_id=0, has_side_effects=True, vmem_limit_bytes=48 << 20),
-    )(block_of_slot, face_source, cutoff, state, courant_x, courant_y, table)
+            has_side_effects=True, vmem_limit_bytes=48 << 20),
+    )(block_of_slot, face_source.T, cutoff, state, courant_x, courant_y, table)
     return state + filtered
 
 

time: 90.9 us -> 95.9 us (1.055)
  Pallas kernels: 83.8 us -> 89.4 us
    pallas_call x1, Pallas kernels: 83.8 us -> 89.4 us  [shards(): pl.pallas_call(step_kernel, out_shape=jax.ShapeDtypeStruct((F, S, NR, L,...]
    unnamed x11 -> x12, local copies, waits for them, and re-layouts: 5.17 us -> 5.08 us
where the time goes in v2:
time: 95.9 us; the launch traced here: 95.6 us
  Pallas kernels  89.4 us (93%)
  local copies, waits for them, and re-layouts  5.08 us (5%)
  other arithmetic  1.09 us (1%)
    pallas_call x1, Pallas kernels, shards(): pl.pallas_call(step_kernel, out_shape=jax.ShapeDtypeStruct((F, S, NR, L,...  89.4 us
    unnamed x12, local copies, waits for them, and re-layouts  5.08 us

profile of v2, /device:TPU:1, one launch (start us, length us, event | category | flops | bytes accessed | tf_op | source)
XLA Modules:
  0.0 95.6 jit_solution(3258984149403850010)
XLA Ops:
  0.0 0.0 copy-start
  0.0 1.2 %copy-done = f32[5,3,8,8,180]{4,3,2,1,0:T(8,128)S(1)} copy-done((f32[5,3,8,8,180]{4,3,2,1,0:T(8,128)S(1)}, f32[5,3,8,8,180]{4,3,2,1,0:T(8,128)}, u32[]{:S(2)}) %copy-start) | copy-done | bytes 691224
  1.2 0.0 copy-start.1
  1.2 0.9 copy-done.1
  2.1 0.0 copy-start.2
  2.1 0.9 copy-done.2
  3.1 0.0 copy-start.3
  3.1 0.7 copy-done.3
  3.8 0.0 copy-start.4
  3.8 0.7 copy-done.4
  4.4 0.0 copy-start.5
  4.4 0.7 copy-done.5
  5.1 89.4 %shard_map.73 = f32[5,3,8,8,180]{4,3,2,1,0:T(8,128)S(1)} custom-call(s32[3]{0:T(128)S(1)} %copy-done.5, s32[2,3]{1,0:T(2,128)S(1)} %bitcast.1, s32[1152]{0:T(1024)S(1)} %copy-done.3, f32[5,3,8,8,180]{4,3,2,1,0:T(8,128)S(1)} %copy-done, f32[3,8,8,180]{3,2,1,0:T(8,128)S(1)} %copy-done.1, f32[3,8,8,180]{3,2,1,0:T(8,128)S(1)} %copy-done.2, ...), custom_call_target="tpu_custom_call" | custom-call | tf_op jit(solution)/shard_map/pallas_call | solution.py:346
  94.5 1.1 %add.3 = f32[5,3,8,8,180]{4,3,2,1,0:T(8,128)} add(f32[5,3,8,8,180]{4,3,2,1,0:T(8,128)S(1)} %copy-done, f32[5,3,8,8,180]{4,3,2,1,0:T(8,128)S(1)} %shard_map.73) | non-fusion elementwise | flops 172800 | bytes 2073600 | tf_op jit(solution)/shard_map/add | solution.py:387
Async XLA Ops:
  0.0 1.2 %copy-start = (f32[5,3,8,8,180]{4,3,2,1,0:T(8,128)S(1)}, f32[5,3,8,8,180]{4,3,2,1,0:T(8,128)}, u32[]{:S(2)}) copy-start(f32[5,3,8,8,180]{4,3,2,1,0:T(8,128)} %state_in.1) | copy-start | bytes 2073604
  1.2 0.9 copy-start.1
  2.1 0.9 copy-start.2
  3.1 0.7 copy-start.3
  3.8 0.7 copy-start.4
  4.4 0.7 copy-start.5

commit v3 on v2

--- a/solution.py
+++ b/solution.py
@@ -15,6 +15,7 @@
 LANES = 256
 NLAT, NLONDEV, HALF = 48, 16, 8
 PIECES = NLAT * 8
+INNER, ROWS = 64, 88
 MESH = pl.DeviceIdType.MESH
 HIGHEST = lax.Precision.HIGHEST
 
@@ -93,6 +94,16 @@
     half, seat = lon // HALF, lon % HALF
     partner = (lon + HALF) % NLONDEV
     east, west = (lon + 1) % NLONDEV, (lon + NLONDEV - 1) % NLONDEV
+
+    barrier = pltpu.get_barrier_semaphore()
+
+    @pl.loop(1, NLAT)
+    def _(i):
+        pl.semaphore_signal(barrier, inc=1, device_id={"lat": (lat + i) % NLAT}, device_id_type=MESH)
+
+    @pl.loop(1, NLONDEV)
+    def _(i):
+        pl.semaphore_signal(barrier, inc=1, device_id={"lon": (lon + i) % NLONDEV}, device_id_type=MESH)
 
     loads = [
         pltpu.make_async_copy(source, target, load_sem.at[i])
@@ -158,14 +169,8 @@
         pick, cx_ref[...].reshape(S * NR * L, W), (((1,), (1,)), ((), ())),
         precision=HIGHEST, preferred_element_type=jnp.float32)
 
-    def piece(ref, i):
-        return ref.at[pl.ds(pl.multiple_of(i * 16, 16), 9), :]
-
-    @pl.loop(1, NLAT)
-    def _(i):
-        to = (lat + i) % NLAT
-        pltpu.make_async_remote_copy(
-            piece(send1, to), piece(got1, lat), s1, r1, device_id={"lat": to}, device_id_type=MESH).start()
+    rows_out[...] = jnp.zeros_like(rows_out)
+    pl.semaphore_wait(barrier, NLAT - 1 + NLONDEV - 1)
 
     to_west = pltpu.make_async_remote_copy(
         edges, from_east, edge_send.at[0], edge_recv.at[0], device_id={"lon": west}, device_id_type=MESH)
@@ -173,29 +178,25 @@
         edges, from_west, edge_send.at[1], edge_recv.at[1], device_id={"lon": east}, device_id_type=MESH)
     to_west.start()
     to_east.start()
-    mine = pl.ds(pl.multiple_of(lat * 16, 16), 16)
-    got1[mine, :] = send1[mine, :]
+
+    def piece(ref, i):
+        return ref.at[pl.ds(pl.multiple_of(i * 16, 16), 9), :]
+
+    def send_pieces(source, target, send_sem, recv_sem):
+        @pl.loop(1, NLAT)
+        def _(i):
+            to = (lat + i) % NLAT
+            pltpu.make_async_remote_copy(
+                piece(source, to), piece(target, lat), send_sem, recv_sem,
+                device_id={"lat": to}, device_id_type=MESH).start()
 
     def wait_pieces(sem, ref):
         whole = ref.at[pl.ds(0, 9 * (NLAT - 1)), :]
         pltpu.make_async_copy(whole, whole, sem).wait()
 
-    wait_pieces(r1, got1)
-    pieces = jnp.concatenate(unpack(got1[...]), axis=1)
-    asked = jnp.broadcast_to(pieces[:, W:W + 1], (PIECES, PIECES))
-    onehot = jnp.where(asked == iota((PIECES, PIECES), 1).astype(jnp.float32), 1.0, 0.0).astype(jnp.bfloat16)
-    a, b, c = split3(pieces)
-    nn = ((1,), (0,))
-    found = (dot(onehot, a, nn) + dot(onehot, b, nn)) + dot(onehot, c, nn)
-    send2[...] = pack(found[:, :128], found[:, 128:])
-
-    @pl.loop(1, NLAT)
-    def _(i):
-        to = (lat + i) % NLAT
-        pltpu.make_async_remote_copy(
-            piece(send2, to), piece(halo, lat), s2, r2, device_id={"lat": to}, device_id_type=MESH).start()
-
-    halo[mine, :] = send2[mine, :]
+    mine = pl.ds(pl.multiple_of(lat * 16, 16), 16)
+    send_pieces(send1, got1, s1, r1)
+    got1[mine, :] = send1[mine, :]
 
     to_west.wait()
     to_east.wait()
@@ -206,11 +207,153 @@
         from_east[...], place(0, W - 1), tn, precision=HIGHEST, preferred_element_type=jnp.float32)
     west_in[...] = lax.dot_general(
         from_west[...], place(1, 0), tn, precision=HIGHEST, preferred_element_type=jnp.float32)
+
+    zeros = jnp.zeros((L, LANES - W), jnp.float32)
+
+    def at_row(f, s, r):
+        return pl.ds(pl.multiple_of(((f * S + s) * NR + r) * L, L), L)
+
+    def tend_row(f, s, r):
+        return pl.ds(pl.multiple_of(((s * F + f) * NR + r) * L, L), L)
+
+    def put_tendency(f, s, r, here, merid):
+        at = at_row(f, s, r)
+        zonal = jnp.concatenate([cx_ref[s, r], zeros], axis=1)
+        to_the_east = jnp.where(lane == W - 1, east_in[at, :], pltpu.roll(here, LANES - 1, 1))
+        across = zonal * (here + to_the_east) * 0.5
+        cw = west_in[pl.ds(1024 + (s * NR + r) * L, L), :]
+        from_the_west = jnp.where(lane == 0, cw * (west_in[at, :] + here) * 0.5, pltpu.roll(across, 1, 1))
+        tend[tend_row(f, s, r), :] = jnp.where(lane < W, -((across - from_the_west) + merid), 0.0)
+
+    def wind(s, r):
+        return jnp.concatenate([cy_ref[s, r], zeros], axis=1)
+
+    for s in range(S):
+        @pl.loop(0, F)
+        def _(f):
+            here = tile(f, s, 1)
+            flux = wind(s, 0) * (tile(f, s, 0) + here) * 0.5
+            for r in range(1, NR - 1):
+                after = tile(f, s, r + 1)
+                next_flux = wind(s, r) * (here + after) * 0.5
+                put_tendency(f, s, r, here, next_flux - flux)
+                flux, here = next_flux, after
+
+    def spot(r, k, f):
+        if 0 < r < NR - 1:
+            n = ((r - 1) * 2 + k) * F + f
+            return (n // 8) * ROWS + (n % 8) * L
+        n = ((r // (NR - 1)) * 2 + k) * F + f
+        return (n // 3) * ROWS + INNER + (n % 3) * L
+
+    def spot_rows(r, k, f):
+        return pl.ds(pl.multiple_of(spot(r, k, f), L), L)
+
+    uppers = [jnp.full((L, LANES), picks[k], jnp.int32) == k + 1 for k in range(2)]
+
+    def gather_rows(rs):
+        for k in range(2):
+            @pl.loop(0, F)
+            def _(f):
+                for r in rs:
+                    low, high = tend[tend_row(f, k, r), :], tend[tend_row(f, k + 1, r), :]
+                    rows_out[spot_rows(r, k, f), :] = jnp.where(uppers[k], high, low)
+
+    starts, sizes = (0, INNER), (INNER, ROWS - INNER)
+
+    def part(g, i):
+        return pl.ds(pl.multiple_of(i * ROWS + starts[g], L), sizes[g])
+
+    def seat_copy(g, i, source, target, send_sem, recv_sem):
+        to = (seat + i) % HALF
+        return pltpu.make_async_remote_copy(
+            source.at[part(g, to), :], target.at[part(g, seat), :], send_sem.at[g, to], recv_sem.at[g, seat],
+            device_id={"lon": half * HALF + to}, device_id_type=MESH)
+
+    def seat_wait(g, i, source, target, send_sem, recv_sem):
+        other = (seat + HALF - i) % HALF
+        pltpu.make_async_remote_copy(
+            source.at[part(g, other), :], target.at[part(g, other), :], send_sem.at[g, other],
+            recv_sem.at[g, other], device_id={"lon": half * HALF + other}, device_id_type=MESH).wait_recv()
+
+    there = (rows_out, rows_in, a_send, a_recv)
+    back = (smooth_out, smooth_in, b_send, b_recv)
+
+    def exchange(g, way):
+        for i in range(1, HALF):
+            seat_copy(g, i, *way).start()
+        way[1][part(g, seat), :] = way[0][part(g, seat), :]
+
+    def arrive(g, way):
+        for i in range(1, HALF):
+            seat_wait(g, i, *way)
+
+    def leave(g, way):
+        for i in range(1, HALF):
+            seat_copy(g, i, *way).wait_send()
+
+    nn, nt = ((1,), (0,)), ((1,), (1,))
+
+    def forward(g):
+        total = jnp.zeros((sizes[g], 2 * KCUT), jnp.float32)
+        for d in range(HALF):
+            xh, xl = split2(rows_in[d * ROWS + starts[g]:d * ROWS + starts[g] + sizes[g], :])
+            total += dot(xh, table[0, d], nn) + (dot(xl, table[0, d], nn) + dot(xh, table[1, d], nn))
+        spec[starts[g]:starts[g] + sizes[g], :] = total
+
+    def swap(g):
+        rows = pl.ds(starts[g], sizes[g])
+        return pltpu.make_async_remote_copy(
+            spec.at[rows, :], spec_in.at[rows, :], y_send.at[g], y_recv.at[g],
+            device_id={"lon": partner}, device_id_type=MESH)
+
+    chosen = [jnp.where(picks[k] == k + 1, blocks[k + 1], blocks[k]) for k in range(2)]
+
+    def limits(g):
+        parts = []
+        for j in range(sizes[g] // L):
+            if g == 0:
+                n = seat * 8 + j
+                r = 1 + n // (2 * F)
+            else:
+                n = seat * 3 + j
+                r = jnp.minimum(n // (2 * F), 1) * (NR - 1)
+            block = jnp.where((n // F) % 2 == 0, chosen[0], chosen[1])
+            parts.append(jnp.full((L, 2 * KCUT), cut_ref[block * NR + r], jnp.int32))
+        return jnp.concatenate(parts, axis=0)
+
+    def inverse(g):
+        shape = (sizes[g], 2 * KCUT)
+        wave = iota(shape, 1) % KCUT
+        sign = jnp.where(wave % 2 == 0, 1.0, -1.0)
+        scale = jnp.where(wave == 0, 1.0 / NLON, 2.0 / NLON)
+        rows = slice(starts[g], starts[g] + sizes[g])
+        weights = jnp.where(wave < limits(g), scale, 0.0)
+        xh, xl = split2((spec[rows, :] + sign * spec_in[rows, :]) * weights)
+        for d in range(HALF):
+            smooth_out[d * ROWS + starts[g]:d * ROWS + starts[g] + sizes[g], :] = dot(xh, table[0, d], nt) + (
+                dot(xl, table[0, d], nt) + dot(xh, table[1, d], nt))
+
+    gather_rows(range(1, NR - 1))
+    exchange(0, there)
+
+    wait_pieces(r1, got1)
+    pieces = jnp.concatenate(unpack(got1[...]), axis=1)
+    asked = jnp.broadcast_to(pieces[:, W:W + 1], (PIECES, PIECES))
+    onehot = jnp.where(asked == iota((PIECES, PIECES), 1).astype(jnp.float32), 1.0, 0.0).astype(jnp.bfloat16)
+    a, b, c = split3(pieces)
+    found = (dot(onehot, a, nn) + dot(onehot, b, nn)) + dot(onehot, c, nn)
+    send2[...] = pack(found[:, :128], found[:, 128:])
+    send_pieces(send2, halo, s2, r2)
+    halo[mine, :] = send2[mine, :]
+
+    load_table.wait()
+    arrive(0, there)
+    forward(0)
+    swap(0).start()
+
     wait_pieces(r2, halo)
     main[...], tail[...] = unpack(halo[...])
-
-    zeros = jnp.zeros((L, LANES - W), jnp.float32)
-
     for s in range(S):
         kept = jnp.full((L, LANES), keep[s], jnp.float32)
 
@@ -218,123 +361,53 @@
         def _(f):
             above, below = load_rows(main, tail, f, s), load_rows(main, tail, f, S + s)
             north_wind = load_rows(main, tail, F, s)
-            here = tile(f, s, 0)
-            flux = north_wind * (above + here) * 0.5
-            for r in range(NR):
-                at = pl.ds(pl.multiple_of(((f * S + s) * NR + r) * L, L), L)
-                wind = jnp.concatenate([cy_ref[s, r], zeros], axis=1)
-                zonal = jnp.concatenate([cx_ref[s, r], zeros], axis=1)
-                after = tile(f, s, r + 1) if r < NR - 1 else below
-                next_flux = wind * (here + after) * 0.5
-                if r == NR - 1:
-                    next_flux = next_flux * kept
-                to_the_east = jnp.where(lane == W - 1, east_in[at, :], pltpu.roll(here, LANES - 1, 1))
-                across = zonal * (here + to_the_east) * 0.5
-                cw = west_in[pl.ds(1024 + (s * NR + r) * L, L), :]
-                from_the_west = jnp.where(
-                    lane == 0, cw * (west_in[at, :] + here) * 0.5, pltpu.roll(across, 1, 1))
-                value = -((across - from_the_west) + (next_flux - flux))
-                tend[pl.ds(pl.multiple_of(((s * F + f) * NR + r) * L, L), L), :] = jnp.where(lane < W, value, 0.0)
-                flux, here = next_flux, after
-
-    for k in range(2):
-        upper = jnp.full((L, LANES), picks[k], jnp.int32) == k + 1
-
-        @pl.loop(0, F)
-        def _(f):
-            for r in range(NR):
-                low, high = [
-                    tend[pl.ds(pl.multiple_of(((s * F + f) * NR + r) * L, L), L), :] for s in (k, k + 1)]
-                rows_out[r, k, pl.ds(pl.multiple_of(f * L, L), L), :] = jnp.where(upper, high, low)
-
-    def out_copy(k, i):
-        to = (seat + i) % HALF
-        return pltpu.make_async_remote_copy(
-            rows_out.at[to, k], rows_in.at[seat, k], a_send.at[k, to], a_recv.at[k, seat],
-            device_id={"lon": half * HALF + to}, device_id_type=MESH)
-
-    def in_wait(k, i):
-        source = (seat + HALF - i) % HALF
-        pltpu.make_async_remote_copy(
-            rows_out.at[source, k], rows_in.at[source, k], a_send.at[k, source], a_recv.at[k, source],
-            device_id={"lon": half * HALF + source}, device_id_type=MESH).wait_recv()
-
-    for k in range(2):
-        for i in range(1, HALF):
-            out_copy(k, i).start()
-    rows_in[seat] = rows_out[seat]
-    load_table.wait()
-
-    def forward(k):
-        for i in range(1, HALF):
-            in_wait(k, i)
-        total = jnp.zeros((F * L, 2 * KCUT), jnp.float32)
-        for d in range(HALF):
-            xh, xl = split2(rows_in[d, k])
-            total += dot(xh, table[0, d], nn) + (dot(xl, table[0, d], nn) + dot(xh, table[1, d], nn))
-        spec[k] = total
-
-    def swap(k):
-        return pltpu.make_async_remote_copy(
-            spec.at[k], spec_in.at[k], y_send.at[k], y_recv.at[k], device_id={"lon": partner}, device_id_type=MESH)
-
-    for k in range(2):
-        forward(k)
-        swap(k).start()
-
-    wave = iota((F * L, 2 * KCUT), 1) % KCUT
-    sign = jnp.where(wave % 2 == 0, 1.0, -1.0)
-    scale = jnp.where(wave == 0, 1.0 / NLON, 2.0 / NLON)
-    nt = ((1,), (1,))
-
-    def back_copy(k, i):
-        to = (seat + i) % HALF
-        return pltpu.make_async_remote_copy(
-            smooth_out.at[to, k], smooth_in.at[seat, k], b_send.at[k, to], b_recv.at[k, seat],
-            device_id={"lon": half * HALF + to}, device_id_type=MESH)
-
-    def back_wait(k, i):
-        source = (seat + HALF - i) % HALF
-        pltpu.make_async_remote_copy(
-            smooth_out.at[source, k], smooth_in.at[source, k], b_send.at[k, source], b_recv.at[k, source],
-            device_id={"lon": half * HALF + source}, device_id_type=MESH).wait_recv()
-
-    for k in range(2):
-        swap(k).wait()
-        block = jnp.where(picks[k] == k + 1, blocks[k + 1], blocks[k])
-        limit = cut_ref[block * NR + seat]
-        kept = jnp.where(wave < jnp.full(wave.shape, limit, jnp.int32), scale, 0.0)
-        xh, xl = split2((spec[k] + sign * spec_in[k]) * kept)
-        for d in range(HALF):
-            smooth_out[d, k] = dot(xh, table[0, d], nt) + (dot(xl, table[0, d], nt) + dot(xh, table[1, d], nt))
-        for i in range(1, HALF):
-            back_copy(k, i).start()
-        smooth_in[seat, k] = smooth_out[seat, k]
-
-    for k in range(2):
-        for i in range(1, HALF):
-            back_wait(k, i)
-
-    for s in range(S):
-        use = [
-            jnp.full((L, LANES), jnp.where(picks[k] == s, polar[s], 0), jnp.int32) > 0
-            for k in range(2)
-        ]
-
-        @pl.loop(0, F)
-        def _(f):
-            for r in range(NR):
-                value = tend[pl.ds(pl.multiple_of(((s * F + f) * NR + r) * L, L), L), :]
-                for k in range(2):
-                    value = jnp.where(use[k], smooth_in[r, k, pl.ds(pl.multiple_of(f * L, L), L), :], value)
-                out_ref[f, s, r] = value[:, :W]
+            here, after = tile(f, s, 0), tile(f, s, 1)
+            put_tendency(
+                f, s, 0, here, wind(s, 0) * (here + after) * 0.5 - north_wind * (above + here) * 0.5)
+            before, here = tile(f, s, NR - 2), tile(f, s, NR - 1)
+            put_tendency(
+                f, s, NR - 1, here,
+                wind(s, NR - 1) * (here + below) * 0.5 * kept - wind(s, NR - 2) * (before + here) * 0.5)
+
+    gather_rows((0, NR - 1))
+    exchange(1, there)
+
+    swap(0).wait()
+    inverse(0)
+    exchange(0, back)
+
+    arrive(1, there)
+    forward(1)
+    swap(1).start()
+    swap(1).wait()
+    inverse(1)
+    exchange(1, back)
+
+    uses = [
+        [jnp.full((L, LANES), jnp.where(picks[k] == s, polar[s], 0), jnp.int32) > 0 for k in range(2)]
+        for s in range(S)
+    ]
+
+    def finish(rs):
+        for s in range(S):
+            @pl.loop(0, F)
+            def _(f):
+                for r in rs:
+                    value = tend[tend_row(f, s, r), :]
+                    for k in range(2):
+                        value = jnp.where(uses[s][k], smooth_in[spot_rows(r, k, f), :], value)
+                    out_ref[f, s, r] = value[:, :W]
+
+    arrive(0, back)
+    finish(range(1, NR - 1))
+    arrive(1, back)
+    finish((0, NR - 1))
 
     wait_pieces(s1, send1)
     wait_pieces(s2, send2)
-    for k in range(2):
-        for i in range(1, HALF):
-            out_copy(k, i).wait_send()
-            back_copy(k, i).wait_send()
+    for g in range(2):
+        leave(g, there)
+        leave(g, back)
 
 
 def shards(table, state, courant_x, courant_y, block_of_slot, face_source, cutoff):
@@ -369,12 +442,12 @@
             pltpu.VMEM((1280, LANES), f32),
             pltpu.VMEM((1280, LANES), f32),
             pltpu.VMEM((rows, LANES), f32),
-            pltpu.VMEM((NR, 2, F * L, LANES), f32),
-            pltpu.VMEM((NR, 2, F * L, LANES), f32),
-            pltpu.VMEM((2, F * L, 2 * KCUT), f32),
-            pltpu.VMEM((2, F * L, 2 * KCUT), f32),
-            pltpu.VMEM((NR, 2, F * L, LANES), f32),
-            pltpu.VMEM((NR, 2, F * L, LANES), f32),
+            pltpu.VMEM((HALF * ROWS, LANES), f32),
+            pltpu.VMEM((HALF * ROWS, LANES), f32),
+            pltpu.VMEM((ROWS, 2 * KCUT), f32),
+            pltpu.VMEM((ROWS, 2 * KCUT), f32),
+            pltpu.VMEM((HALF * ROWS, LANES), f32),
+            pltpu.VMEM((HALF * ROWS, LANES), f32),
             dma((6,)), dma, dma, dma, dma, dma,
             dma((2,)), dma((2,)),
             dma((2, HALF)), dma((2, HALF)),
@@ -382,7 +455,7 @@
             dma((2, HALF)), dma((2, HALF)),
         ],
         compiler_params=pltpu.CompilerParams(
-            has_side_effects=True, vmem_limit_bytes=48 << 20),
+            collective_id=0, has_side_effects=True, vmem_limit_bytes=48 << 20),
     )(block_of_slot, face_source.T, cutoff, state, courant_x, courant_y, table)
     return state + filtered
 

time: 95.9 us -> 72.6 us (0.76)
  Pallas kernels: 89.4 us -> 65.9 us
    pallas_call x1, Pallas kernels: 89.4 us -> 65.9 us  [shards(): pl.pallas_call(step_kernel, out_shape=jax.ShapeDtypeStruct((F, S, NR, L,...]
where the time goes in v3:
time: 72.6 us; the launch traced here: 72.1 us
  Pallas kernels  65.9 us (91%)
  local copies, waits for them, and re-layouts  5.08 us (7%)
  other arithmetic  1.09 us (2%)
    pallas_call x1, Pallas kernels, shards(): pl.pallas_call(step_kernel, out_shape=jax.ShapeDtypeStruct((F, S, NR, L,...  65.9 us
    unnamed x12, local copies, waits for them, and re-layouts  5.08 us

profile of v3, /device:TPU:1, one launch (start us, length us, event | category | flops | bytes accessed | tf_op | source)
XLA Modules:
  0.0 72.1 jit_solution(17579923915908570594)
XLA Ops:
  0.0 0.0 copy-start
  0.0 1.2 %copy-done = f32[5,3,8,8,180]{4,3,2,1,0:T(8,128)S(1)} copy-done((f32[5,3,8,8,180]{4,3,2,1,0:T(8,128)S(1)}, f32[5,3,8,8,180]{4,3,2,1,0:T(8,128)}, u32[]{:S(2)}) %copy-start) | copy-done | bytes 691224
  1.2 0.0 copy-start.1
  1.2 0.9 %copy-done.1 = f32[3,8,8,180]{3,2,1,0:T(8,128)S(1)} copy-done((f32[3,8,8,180]{3,2,1,0:T(8,128)S(1)}, f32[3,8,8,180]{3,2,1,0:T(8,128)}, u32[]{:S(2)}) %copy-start.1) | copy-done | bytes 138264
  2.1 0.0 copy-start.2
  2.1 0.9 %copy-done.2 = f32[3,8,8,180]{3,2,1,0:T(8,128)S(1)} copy-done((f32[3,8,8,180]{3,2,1,0:T(8,128)S(1)}, f32[3,8,8,180]{3,2,1,0:T(8,128)}, u32[]{:S(2)}) %copy-start.2) | copy-done | bytes 138264
  3.1 0.0 copy-start.3
  3.1 0.7 copy-done.3
  3.8 0.0 copy-start.4
  3.8 0.7 copy-done.4
  4.4 0.0 copy-start.5
  4.4 0.7 copy-done.5
  5.1 65.9 %shard_map.73 = f32[5,3,8,8,180]{4,3,2,1,0:T(8,128)S(1)} custom-call(s32[3]{0:T(128)S(1)} %copy-done.5, s32[2,3]{1,0:T(2,128)S(1)} %bitcast.1, s32[1152]{0:T(1024)S(1)} %copy-done.3, f32[5,3,8,8,180]{4,3,2,1,0:T(8,128)S(1)} %copy-done, f32[3,8,8,180]{3,2,1,0:T(8,128)S(1)} %copy-done.1, f32[3,8,8,180]{3,2,1,0:T(8,128)S(1)} %copy-done.2, ...), custom_call_target="tpu_custom_call" | custom-call | tf_op jit(solution)/shard_map/pallas_call | solution.py:419
  71.0 1.1 %add.3 = f32[5,3,8,8,180]{4,3,2,1,0:T(8,128)} add(f32[5,3,8,8,180]{4,3,2,1,0:T(8,128)S(1)} %copy-done, f32[5,3,8,8,180]{4,3,2,1,0:T(8,128)S(1)} %shard_map.73) | non-fusion elementwise | flops 172800 | bytes 2073600 | tf_op jit(solution)/shard_map/add | solution.py:460
Async XLA Ops:
  0.0 1.2 %copy-start = (f32[5,3,8,8,180]{4,3,2,1,0:T(8,128)S(1)}, f32[5,3,8,8,180]{4,3,2,1,0:T(8,128)}, u32[]{:S(2)}) copy-start(f32[5,3,8,8,180]{4,3,2,1,0:T(8,128)} %state_in.1) | copy-start | bytes 2073604
  1.2 0.9 %copy-start.1 = (f32[3,8,8,180]{3,2,1,0:T(8,128)S(1)}, f32[3,8,8,180]{3,2,1,0:T(8,128)}, u32[]{:S(2)}) copy-start(f32[3,8,8,180]{3,2,1,0:T(8,128)} %cx_in.1) | copy-start | bytes 414724
  2.1 0.9 %copy-start.2 = (f32[3,8,8,180]{3,2,1,0:T(8,128)S(1)}, f32[3,8,8,180]{3,2,1,0:T(8,128)}, u32[]{:S(2)}) copy-start(f32[3,8,8,180]{3,2,1,0:T(8,128)} %cy_in.1) | copy-start | bytes 414724
  3.1 0.7 copy-start.3
  3.8 0.7 copy-start.4
  4.4 0.7 copy-start.5

commit v4 on v3

--- a/solution.py
+++ b/solution.py
@@ -17,7 +17,6 @@
 PIECES = NLAT * 8
 INNER, ROWS = 64, 88
 MESH = pl.DeviceIdType.MESH
-HIGHEST = lax.Precision.HIGHEST
 
 
 def basis_table():
@@ -49,11 +48,6 @@
 def store_rows(main, tail, c, t, value):
     main[pl.ds(c * 64 + t, L, stride=8), :] = value[:, :128]
     tail[pl.ds(c * 64 + t, L, stride=8), :] = value[:, 128:]
-
-
-def load_rows(main, tail, c, t):
-    at = pl.ds(c * 64 + t, L, stride=8)
-    return jnp.concatenate([main[at, :], tail[at, :]], axis=1)
 
 
 def pack(main, tail):
@@ -77,6 +71,29 @@
     return main.reshape(PIECES, 128), tail.reshape(PIECES, 128)
 
 
+def pack_asked(main, tail):
+    shape = (NLAT, 8, 128)
+    main, tail = main.reshape(shape), tail.reshape(shape)
+    sub, lane = iota(shape, 1), iota(shape, 2)
+    low = lane < 64
+
+    def tails(north, south):
+        return jnp.where(low, pltpu.roll(tail, north, 1), pltpu.roll(pltpu.roll(tail, south, 1), 64, 2))
+
+    first = jnp.where(sub < 2, main, jnp.where(sub < 4, pltpu.roll(main, 7, 1), tails(4, 1)))
+    second = jnp.where(
+        sub < 1, pltpu.roll(main, 6, 1), jnp.where(sub < 2, pltpu.roll(main, 4, 1), tails(0, 5)))
+    return jnp.stack([first, second], axis=1).reshape(2 * PIECES, 128)
+
+
+def load_halo(ref, c, k, south):
+    row, tail_row = (k + 2 * south, 4 + k) if k < 2 else (8 + south, 10)
+    tail = ref[pl.ds(c * 128 + tail_row, L, stride=16), :]
+    if south:
+        tail = pltpu.roll(tail, 64, 1)
+    return jnp.concatenate([ref[pl.ds(c * 128 + row, L, stride=16), :], tail], axis=1)
+
+
 def iota(shape, dim):
     return lax.broadcasted_iota(jnp.int32, shape, dim)
 
@@ -86,9 +103,9 @@
     out_ref,
     block_ref, face_ref, cut_ref, state_ref, cx_ref, cy_ref,
     table, padded, main, tail, send1, got1, send2, halo,
-    edges, from_west, from_east, east_in, west_in,
+    edges, from_west, from_east,
     tend, rows_out, rows_in, spec, spec_in, smooth_out, smooth_in,
-    load_sem, table_sem, s1, r1, s2, r2, edge_send, edge_recv, a_send, a_recv, y_send, y_recv, b_send, b_recv,
+    load_sem, table_sem, s1, r1, s2, r2, s3, r3, edge_send, edge_recv, a_send, a_recv, y_send, y_recv, b_send, b_recv,
 ):
     lat, lon = lax.axis_index("lat"), lax.axis_index("lon")
     half, seat = lon // HALF, lon % HALF
@@ -113,17 +130,12 @@
     ]
     for load in loads:
         load.start()
-    load_table = pltpu.make_async_copy(table_hbm, table, table_sem)
-    load_table.start()
     main[...] = jnp.zeros_like(main)
     tail[...] = jnp.zeros_like(tail)
-    padded[...] = jnp.zeros_like(padded)
-    edges[...] = jnp.zeros_like(edges)
-    for load in loads:
+    load_table = pltpu.make_async_copy(table_hbm, table, table_sem)
+    for load in loads[:4]:
         load.wait()
 
-    blocks = [block_ref[s] for s in range(S)]
-    polar = [jnp.where(b < POLAR, 1, 0) + jnp.where(b >= NBLK - POLAR, 1, 0) for b in blocks]
     cols, keep = [], []
     for t in range(2 * S):
         n = face_ref[t // S, t % S]
@@ -131,46 +143,80 @@
         cols.append(jnp.where(n >= 0, 8 * lax.div(safe, S) + lax.rem(safe, S) + (t // S) * S, -1))
         keep.append(jnp.where(n >= 0, 1.0, 0.0))
     keep = keep[S:]
+    blocks = [block_ref[s] for s in range(S)]
+    polar = [jnp.where(b < POLAR, 1, 0) + jnp.where(b >= NBLK - POLAR, 1, 0) for b in blocks]
     first = (1 - polar[0]) * polar[2]
-    picks = [first, 1 + polar[2]]
+    picks = [first, 1 + polar[2], 2 - first - polar[2]]
+    asks = [
+        jnp.where(picks[t % S] == 0, cols[t // S * S], jnp.where(picks[t % S] == 1, cols[t // S * S + 1], cols[t // S * S + 2]))
+        for t in range(2 * S)
+    ]
 
     lane = iota((L, LANES), 1)
-
-    padded[:, :W] = state_ref[...].reshape(F * S * NR * L, W)
-
-    def tile(f, s, r):
-        return padded[pl.ds(pl.multiple_of(((f * S + s) * NR + r) * L, L), L), :]
+    zeros = jnp.zeros((L, LANES - W), jnp.float32)
 
     for t in range(2 * S):
         s = t % S
-        want = jnp.full((L, LANES), cols[t].astype(jnp.float32), jnp.float32)
+        want = jnp.full((L, LANES), asks[t].astype(jnp.float32), jnp.float32)
         for f in range(F):
-            row = tile(f, s, NR - 1 if t < S else 0)
+            row = jnp.concatenate([state_ref[f, s, NR - 1 if t < S else 0], zeros], axis=1)
             store_rows(main, tail, f, t, jnp.where(lane == W, want, row))
         if t < S:
-            wind = jnp.concatenate([cy_ref[s, NR - 1], jnp.zeros((L, LANES - W), jnp.float32)], axis=1)
-            store_rows(main, tail, F, t, jnp.where(lane == W, want, wind))
+            last_wind = jnp.concatenate([cy_ref[s, NR - 1], zeros], axis=1)
+            store_rows(main, tail, F, t, jnp.where(lane == W, want, last_wind))
         else:
             store_rows(main, tail, F, t, jnp.where(lane == W, want, 0.0))
 
     send1[...] = pack(main[...], tail[...])
 
-    pick = jnp.where(
-        jnp.logical_or(
-            jnp.logical_and(iota((8, W), 0) == 0, iota((8, W), 1) == 0),
-            jnp.logical_and(iota((8, W), 0) == 1, iota((8, W), 1) == W - 1),
-        ),
-        1.0, 0.0,
-    ).astype(jnp.float32)
-    edges[:, :960] = lax.dot_general(
-        pick, state_ref[...].reshape(F * S * NR * L, W), (((1,), (1,)), ((), ())),
-        precision=HIGHEST, preferred_element_type=jnp.float32)
-    edges[:, 1024:1216] = lax.dot_general(
-        pick, cx_ref[...].reshape(S * NR * L, W), (((1,), (1,)), ((), ())),
-        precision=HIGHEST, preferred_element_type=jnp.float32)
-
-    rows_out[...] = jnp.zeros_like(rows_out)
     pl.semaphore_wait(barrier, NLAT - 1 + NLONDEV - 1)
+
+    def send_pieces(source, target, send_sem, recv_sem, start, size):
+        def piece(ref, i):
+            return ref.at[pl.ds(pl.multiple_of(i * 16 + start, 8), size), :]
+
+        @pl.loop(1, NLAT)
+        def _(i):
+            to = (lat + i) % NLAT
+            pltpu.make_async_remote_copy(
+                piece(source, to), piece(target, lat), send_sem, recv_sem,
+                device_id={"lat": to}, device_id_type=MESH).start()
+
+    def wait_pieces(sem, ref, size):
+        whole = ref.at[pl.ds(0, size * (NLAT - 1)), :]
+        pltpu.make_async_copy(whole, whole, sem).wait()
+
+    mine = pl.ds(pl.multiple_of(lat * 16, 16), 16)
+    send_pieces(send1, got1, s1, r1, 0, 9)
+    got1[mine, :] = send1[mine, :]
+
+    for load in loads[4:]:
+        load.wait()
+    narrow = iota((L, 128), 1)
+
+    def lane_of(f, s, r):
+        return (f * S + s) * NR + r
+
+    def put_edges(f, ends):
+        left, right = ends
+        for s in range(S):
+            for r in range(NR):
+                n = lane_of(f, s, r)
+                row = state_ref[f, s, r]
+                last = jnp.concatenate([row[:, 128:], zeros], axis=1)
+                left = jnp.where(narrow == n, pltpu.roll(row[:, :128], n, 1), left)
+                right = jnp.where(narrow == n, pltpu.roll(last, (n + 128 - (W - 1 - 128)) % 128, 1), right)
+        return left, right
+
+    nothing = jnp.zeros((L, 128), jnp.float32)
+    edges[0], edges[1] = lax.fori_loop(0, F, put_edges, (nothing, nothing))
+    right = nothing
+    for s in range(S):
+        for r in range(NR):
+            n = s * NR + r
+            last = jnp.concatenate([cx_ref[s, r][:, 128:], zeros], axis=1)
+            right = jnp.where(narrow == n, pltpu.roll(last, (n + 128 - (W - 1 - 128)) % 128, 1), right)
+    edges[2] = right
 
     to_west = pltpu.make_async_remote_copy(
         edges, from_east, edge_send.at[0], edge_recv.at[0], device_id={"lon": west}, device_id_type=MESH)
@@ -179,50 +225,31 @@
     to_west.start()
     to_east.start()
 
-    def piece(ref, i):
-        return ref.at[pl.ds(pl.multiple_of(i * 16, 16), 9), :]
-
-    def send_pieces(source, target, send_sem, recv_sem):
-        @pl.loop(1, NLAT)
-        def _(i):
-            to = (lat + i) % NLAT
-            pltpu.make_async_remote_copy(
-                piece(source, to), piece(target, lat), send_sem, recv_sem,
-                device_id={"lat": to}, device_id_type=MESH).start()
-
-    def wait_pieces(sem, ref):
-        whole = ref.at[pl.ds(0, 9 * (NLAT - 1)), :]
-        pltpu.make_async_copy(whole, whole, sem).wait()
-
-    mine = pl.ds(pl.multiple_of(lat * 16, 16), 16)
-    send_pieces(send1, got1, s1, r1)
-    got1[mine, :] = send1[mine, :]
+
+    load_table.start()
+    padded[...] = jnp.zeros_like(padded)
+    padded[:, :W] = state_ref[...].reshape(F * S * NR * L, W)
+    rows_out[...] = jnp.zeros_like(rows_out)
+
+    def tile(f, s, r):
+        return padded[pl.ds(pl.multiple_of(((f * S + s) * NR + r) * L, L), L), :]
 
     to_west.wait()
     to_east.wait()
-    place = lambda src, dst: jnp.where(
-        jnp.logical_and(iota((8, LANES), 0) == src, iota((8, LANES), 1) == dst), 1.0, 0.0).astype(jnp.float32)
-    tn = (((0,), (0,)), ((), ()))
-    east_in[...] = lax.dot_general(
-        from_east[...], place(0, W - 1), tn, precision=HIGHEST, preferred_element_type=jnp.float32)
-    west_in[...] = lax.dot_general(
-        from_west[...], place(1, 0), tn, precision=HIGHEST, preferred_element_type=jnp.float32)
-
-    zeros = jnp.zeros((L, LANES - W), jnp.float32)
-
-    def at_row(f, s, r):
-        return pl.ds(pl.multiple_of(((f * S + s) * NR + r) * L, L), L)
 
     def tend_row(f, s, r):
         return pl.ds(pl.multiple_of(((s * F + f) * NR + r) * L, L), L)
 
     def put_tendency(f, s, r, here, merid):
-        at = at_row(f, s, r)
+        n = lane_of(f, s, r)
         zonal = jnp.concatenate([cx_ref[s, r], zeros], axis=1)
-        to_the_east = jnp.where(lane == W - 1, east_in[at, :], pltpu.roll(here, LANES - 1, 1))
+        beyond = jnp.concatenate([nothing, pltpu.roll(from_east[0], (128 + (W - 1 - 128) - n) % 128, 1)], axis=1)
+        to_the_east = jnp.where(lane == W - 1, beyond, pltpu.roll(here, LANES - 1, 1))
         across = zonal * (here + to_the_east) * 0.5
-        cw = west_in[pl.ds(1024 + (s * NR + r) * L, L), :]
-        from_the_west = jnp.where(lane == 0, cw * (west_in[at, :] + here) * 0.5, pltpu.roll(across, 1, 1))
+        before = pltpu.roll(from_west[1], (128 - n) % 128, 1)
+        cw = pltpu.roll(from_west[2], (128 - s * NR - r) % 128, 1)
+        inflow = jnp.concatenate([cw * (before + here[:, :128]) * 0.5, nothing], axis=1)
+        from_the_west = jnp.where(lane == 0, inflow, pltpu.roll(across, 1, 1))
         tend[tend_row(f, s, r), :] = jnp.where(lane < W, -((across - from_the_west) + merid), 0.0)
 
     def wind(s, r):
@@ -294,11 +321,16 @@
 
     nn, nt = ((1,), (0,)), ((1,), (1,))
 
+    def product(xh, xl, d, dims):
+        rows = xh.shape[0]
+        both = dot(jnp.concatenate([xh, xl], axis=0), table[0, d], dims)
+        return both[:rows] + (both[rows:] + dot(xh, table[1, d], dims))
+
     def forward(g):
         total = jnp.zeros((sizes[g], 2 * KCUT), jnp.float32)
         for d in range(HALF):
             xh, xl = split2(rows_in[d * ROWS + starts[g]:d * ROWS + starts[g] + sizes[g], :])
-            total += dot(xh, table[0, d], nn) + (dot(xl, table[0, d], nn) + dot(xh, table[1, d], nn))
+            total += product(xh, xl, d, nn)
         spec[starts[g]:starts[g] + sizes[g], :] = total
 
     def swap(g):
@@ -331,20 +363,20 @@
         weights = jnp.where(wave < limits(g), scale, 0.0)
         xh, xl = split2((spec[rows, :] + sign * spec_in[rows, :]) * weights)
         for d in range(HALF):
-            smooth_out[d * ROWS + starts[g]:d * ROWS + starts[g] + sizes[g], :] = dot(xh, table[0, d], nt) + (
-                dot(xl, table[0, d], nt) + dot(xh, table[1, d], nt))
+            smooth_out[d * ROWS + starts[g]:d * ROWS + starts[g] + sizes[g], :] = product(xh, xl, d, nt)
 
     gather_rows(range(1, NR - 1))
     exchange(0, there)
 
-    wait_pieces(r1, got1)
+    wait_pieces(r1, got1, 9)
     pieces = jnp.concatenate(unpack(got1[...]), axis=1)
     asked = jnp.broadcast_to(pieces[:, W:W + 1], (PIECES, PIECES))
     onehot = jnp.where(asked == iota((PIECES, PIECES), 1).astype(jnp.float32), 1.0, 0.0).astype(jnp.bfloat16)
     a, b, c = split3(pieces)
     found = (dot(onehot, a, nn) + dot(onehot, b, nn)) + dot(onehot, c, nn)
-    send2[...] = pack(found[:, :128], found[:, 128:])
-    send_pieces(send2, halo, s2, r2)
+    send2[...] = pack_asked(found[:, :128], found[:, 128:])
+    send_pieces(send2, halo, s2, r2, 0, 6)
+    send_pieces(send2, halo, s3, r3, 8, 3)
     halo[mine, :] = send2[mine, :]
 
     load_table.wait()
@@ -352,23 +384,31 @@
     forward(0)
     swap(0).start()
 
-    wait_pieces(r2, halo)
-    main[...], tail[...] = unpack(halo[...])
-    for s in range(S):
-        kept = jnp.full((L, LANES), keep[s], jnp.float32)
-
-        @pl.loop(0, F)
-        def _(f):
-            above, below = load_rows(main, tail, f, s), load_rows(main, tail, f, S + s)
-            north_wind = load_rows(main, tail, F, s)
-            here, after = tile(f, s, 0), tile(f, s, 1)
-            put_tendency(
-                f, s, 0, here, wind(s, 0) * (here + after) * 0.5 - north_wind * (above + here) * 0.5)
-            before, here = tile(f, s, NR - 2), tile(f, s, NR - 1)
-            put_tendency(
-                f, s, NR - 1, here,
-                wind(s, NR - 1) * (here + below) * 0.5 * kept - wind(s, NR - 2) * (before + here) * 0.5)
-
+    at_pick = [[jnp.full((L, LANES), picks[k], jnp.int32) == s for k in range(S)] for s in range(S)]
+
+    def outer_rows(known):
+        for s in range(S):
+            kept = jnp.full((L, LANES), keep[s], jnp.float32)
+
+            def halo_row(c, south):
+                row = load_halo(halo, c, 1, south)
+                for k in known:
+                    row = jnp.where(at_pick[s][k], load_halo(halo, c, k, south), row)
+                return row
+
+            @pl.loop(0, F)
+            def _(f):
+                above, below, north_wind = halo_row(f, 0), halo_row(f, 1), halo_row(F, 0)
+                here, after = tile(f, s, 0), tile(f, s, 1)
+                put_tendency(
+                    f, s, 0, here, wind(s, 0) * (here + after) * 0.5 - north_wind * (above + here) * 0.5)
+                before, here = tile(f, s, NR - 2), tile(f, s, NR - 1)
+                put_tendency(
+                    f, s, NR - 1, here,
+                    wind(s, NR - 1) * (here + below) * 0.5 * kept - wind(s, NR - 2) * (before + here) * 0.5)
+
+    wait_pieces(r2, halo, 6)
+    outer_rows((0,))
     gather_rows((0, NR - 1))
     exchange(1, there)
 
@@ -379,6 +419,8 @@
     arrive(1, there)
     forward(1)
     swap(1).start()
+    wait_pieces(r3, halo, 3)
+    outer_rows((0, 2))
     swap(1).wait()
     inverse(1)
     exchange(1, back)
@@ -403,8 +445,9 @@
     arrive(1, back)
     finish((0, NR - 1))
 
-    wait_pieces(s1, send1)
-    wait_pieces(s2, send2)
+    wait_pieces(s1, send1, 9)
+    wait_pieces(s2, send2, 6)
+    wait_pieces(s3, send2, 3)
     for g in range(2):
         leave(g, there)
         leave(g, back)
@@ -436,11 +479,9 @@
             pltpu.VMEM((2 * PIECES, 128), f32),
             pltpu.VMEM((2 * PIECES, 128), f32),
             pltpu.VMEM((2 * PIECES, 128), f32),
-            pltpu.VMEM((8, 1280), f32),
-            pltpu.VMEM((8, 1280), f32),
-            pltpu.VMEM((8, 1280), f32),
-            pltpu.VMEM((1280, LANES), f32),
-            pltpu.VMEM((1280, LANES), f32),
+            pltpu.VMEM((3, L, 128), f32),
+            pltpu.VMEM((3, L, 128), f32),
+            pltpu.VMEM((3, L, 128), f32),
             pltpu.VMEM((rows, LANES), f32),
             pltpu.VMEM((HALF * ROWS, LANES), f32),
             pltpu.VMEM((HALF * ROWS, LANES), f32),
@@ -448,7 +489,7 @@
             pltpu.VMEM((ROWS, 2 * KCUT), f32),
             pltpu.VMEM((HALF * ROWS, LANES), f32),
             pltpu.VMEM((HALF * ROWS, LANES), f32),
-            dma((6,)), dma, dma, dma, dma, dma,
+            dma((6,)), dma, dma, dma, dma, dma, dma, dma,
             dma((2,)), dma((2,)),
             dma((2, HALF)), dma((2, HALF)),
             dma((2,)), dma((2,)),

time: 72.6 us -> 70.3 us (0.968)
  the two profiles are of different devices: /device:TPU:1 before, /device:TPU:9 now
where the time goes in v4:
time: 70.3 us; the launch traced here: 70 us
  Pallas kernels  63.8 us (91%)
  local copies, waits for them, and re-layouts  5.08 us (7%)
  other arithmetic  1.09 us (2%)
    pallas_call x1, Pallas kernels, shards(): pl.pallas_call(step_kernel, out_shape=jax.ShapeDtypeStruct((F, S, NR, L,...  63.8 us
    unnamed x12, local copies, waits for them, and re-layouts  5.08 us

profile of v4, /device:TPU:9, one launch (start us, length us, event | category | flops | bytes accessed | tf_op | source)
XLA Modules:
  0.0 70.0 jit_solution(25150798486955873)
XLA Ops:
  0.0 0.0 copy-start
  0.0 1.2 %copy-done = f32[5,3,8,8,180]{4,3,2,1,0:T(8,128)S(1)} copy-done((f32[5,3,8,8,180]{4,3,2,1,0:T(8,128)S(1)}, f32[5,3,8,8,180]{4,3,2,1,0:T(8,128)}, u32[]{:S(2)}) %copy-start) | copy-done | bytes 691224
  1.2 0.0 copy-start.1
  1.2 0.9 %copy-done.1 = f32[3,8,8,180]{3,2,1,0:T(8,128)S(1)} copy-done((f32[3,8,8,180]{3,2,1,0:T(8,128)S(1)}, f32[3,8,8,180]{3,2,1,0:T(8,128)}, u32[]{:S(2)}) %copy-start.1) | copy-done | bytes 138264
  2.1 0.0 copy-start.2
  2.1 0.9 %copy-done.2 = f32[3,8,8,180]{3,2,1,0:T(8,128)S(1)} copy-done((f32[3,8,8,180]{3,2,1,0:T(8,128)S(1)}, f32[3,8,8,180]{3,2,1,0:T(8,128)}, u32[]{:S(2)}) %copy-start.2) | copy-done | bytes 138264
  3.1 0.0 copy-start.3
  3.1 0.7 copy-done.3
  3.8 0.0 copy-start.4
  3.8 0.7 copy-done.4
  4.4 0.0 copy-start.5
  4.4 0.7 copy-done.5
  5.1 63.8 %shard_map.73 = f32[5,3,8,8,180]{4,3,2,1,0:T(8,128)S(1)} custom-call(s32[3]{0:T(128)S(1)} %copy-done.5, s32[2,3]{1,0:T(2,128)S(1)} %bitcast.1, s32[1152]{0:T(1024)S(1)} %copy-done.3, f32[5,3,8,8,180]{4,3,2,1,0:T(8,128)S(1)} %copy-done, f32[3,8,8,180]{3,2,1,0:T(8,128)S(1)} %copy-done.1, f32[3,8,8,180]{3,2,1,0:T(8,128)S(1)} %copy-done.2, ...), custom_call_target="tpu_custom_call" | custom-call | tf_op jit(solution)/shard_map/pallas_call | solution.py:462
  68.9 1.1 %add.3 = f32[5,3,8,8,180]{4,3,2,1,0:T(8,128)} add(f32[5,3,8,8,180]{4,3,2,1,0:T(8,128)S(1)} %copy-done, f32[5,3,8,8,180]{4,3,2,1,0:T(8,128)S(1)} %shard_map.73) | non-fusion elementwise | flops 172800 | bytes 2073600 | tf_op jit(solution)/shard_map/add | solution.py:501
Async XLA Ops:
  0.0 1.2 %copy-start = (f32[5,3,8,8,180]{4,3,2,1,0:T(8,128)S(1)}, f32[5,3,8,8,180]{4,3,2,1,0:T(8,128)}, u32[]{:S(2)}) copy-start(f32[5,3,8,8,180]{4,3,2,1,0:T(8,128)} %state_in.1) | copy-start | bytes 2073604
  1.2 0.9 %copy-start.1 = (f32[3,8,8,180]{3,2,1,0:T(8,128)S(1)}, f32[3,8,8,180]{3,2,1,0:T(8,128)}, u32[]{:S(2)}) copy-start(f32[3,8,8,180]{3,2,1,0:T(8,128)} %cx_in.1) | copy-start | bytes 414724
  2.1 0.9 %copy-start.2 = (f32[3,8,8,180]{3,2,1,0:T(8,128)S(1)}, f32[3,8,8,180]{3,2,1,0:T(8,128)}, u32[]{:S(2)}) copy-start(f32[3,8,8,180]{3,2,1,0:T(8,128)} %cy_in.1) | copy-start | bytes 414724
  3.1 0.7 copy-start.3
  3.8 0.7 copy-start.4
  4.4 0.7 copy-start.5

commit v5 on v4

--- a/solution.py
+++ b/solution.py
@@ -175,9 +175,11 @@
         def piece(ref, i):
             return ref.at[pl.ds(pl.multiple_of(i * 16 + start, 8), size), :]
 
-        @pl.loop(1, NLAT)
+        @pl.loop(0, NLAT - 1)
         def _(i):
-            to = (lat + i) % NLAT
+            turn = i // 4
+            along = 6 + (1 - 2 * (turn % 2)) * ((turn + 1) // 2)
+            to = ((lat // 12 + 3 - i % 4) % 4) * 12 + (lat % 12 + along) % 12
             pltpu.make_async_remote_copy(
                 piece(source, to), piece(target, lat), send_sem, recv_sem,
                 device_id={"lat": to}, device_id_type=MESH).start()
@@ -376,13 +378,13 @@
     found = (dot(onehot, a, nn) + dot(onehot, b, nn)) + dot(onehot, c, nn)
     send2[...] = pack_asked(found[:, :128], found[:, 128:])
     send_pieces(send2, halo, s2, r2, 0, 6)
-    send_pieces(send2, halo, s3, r3, 8, 3)
     halo[mine, :] = send2[mine, :]
 
     load_table.wait()
     arrive(0, there)
     forward(0)
     swap(0).start()
+    send_pieces(send2, halo, s3, r3, 8, 3)
 
     at_pick = [[jnp.full((L, LANES), picks[k], jnp.int32) == s for k in range(S)] for s in range(S)]
 

time: 70.3 us -> 68.5 us (0.974)
  the two profiles are of different devices: /device:TPU:9 before, /device:TPU:1 now
where the time goes in v5:
time: 68.5 us; the launch traced here: 67.9 us
  Pallas kernels  61.7 us (90%)
  local copies, waits for them, and re-layouts  5.08 us (7%)
  other arithmetic  1.09 us (2%)
    pallas_call x1, Pallas kernels, shards(): pl.pallas_call(step_kernel, out_shape=jax.ShapeDtypeStruct((F, S, NR, L,...  61.7 us
    unnamed x12, local copies, waits for them, and re-layouts  5.08 us

profile of v5, /device:TPU:1, one launch (start us, length us, event | category | flops | bytes accessed | tf_op | source)
XLA Modules:
  0.0 67.9 jit_solution(9112958065017104327)
XLA Ops:
  0.0 0.0 copy-start
  0.0 1.2 %copy-done = f32[5,3,8,8,180]{4,3,2,1,0:T(8,128)S(1)} copy-done((f32[5,3,8,8,180]{4,3,2,1,0:T(8,128)S(1)}, f32[5,3,8,8,180]{4,3,2,1,0:T(8,128)}, u32[]{:S(2)}) %copy-start) | copy-done | bytes 691224
  1.2 0.0 copy-start.1
  1.2 0.9 %copy-done.1 = f32[3,8,8,180]{3,2,1,0:T(8,128)S(1)} copy-done((f32[3,8,8,180]{3,2,1,0:T(8,128)S(1)}, f32[3,8,8,180]{3,2,1,0:T(8,128)}, u32[]{:S(2)}) %copy-start.1) | copy-done | bytes 138264
  2.1 0.0 copy-start.2
  2.1 0.9 %copy-done.2 = f32[3,8,8,180]{3,2,1,0:T(8,128)S(1)} copy-done((f32[3,8,8,180]{3,2,1,0:T(8,128)S(1)}, f32[3,8,8,180]{3,2,1,0:T(8,128)}, u32[]{:S(2)}) %copy-start.2) | copy-done | bytes 138264
  3.1 0.0 copy-start.3
  3.1 0.7 %copy-done.3 = s32[1152]{0:T(1024)S(1)} copy-done((s32[1152]{0:T(1024)S(1)}, s32[1152]{0:T(1024)}, u32[]{:S(2)}) %copy-start.3) | copy-done | bytes 4632
  3.8 0.0 copy-start.4
  3.8 0.7 copy-done.4
  4.4 0.0 copy-start.5
  4.4 0.7 copy-done.5
  5.1 61.7 %shard_map.73 = f32[5,3,8,8,180]{4,3,2,1,0:T(8,128)S(1)} custom-call(s32[3]{0:T(128)S(1)} %copy-done.5, s32[2,3]{1,0:T(2,128)S(1)} %bitcast.1, s32[1152]{0:T(1024)S(1)} %copy-done.3, f32[5,3,8,8,180]{4,3,2,1,0:T(8,128)S(1)} %copy-done, f32[3,8,8,180]{3,2,1,0:T(8,128)S(1)} %copy-done.1, f32[3,8,8,180]{3,2,1,0:T(8,128)S(1)} %copy-done.2, ...), custom_call_target="tpu_custom_call" | custom-call | tf_op jit(solution)/shard_map/pallas_call | solution.py:464
  66.8 1.1 %add.3 = f32[5,3,8,8,180]{4,3,2,1,0:T(8,128)} add(f32[5,3,8,8,180]{4,3,2,1,0:T(8,128)S(1)} %copy-done, f32[5,3,8,8,180]{4,3,2,1,0:T(8,128)S(1)} %shard_map.73) | non-fusion elementwise | flops 172800 | bytes 2073600 | tf_op jit(solution)/shard_map/add | solution.py:503
Async XLA Ops:
  0.0 1.2 %copy-start = (f32[5,3,8,8,180]{4,3,2,1,0:T(8,128)S(1)}, f32[5,3,8,8,180]{4,3,2,1,0:T(8,128)}, u32[]{:S(2)}) copy-start(f32[5,3,8,8,180]{4,3,2,1,0:T(8,128)} %state_in.1) | copy-start | bytes 2073604
  1.2 0.9 %copy-start.1 = (f32[3,8,8,180]{3,2,1,0:T(8,128)S(1)}, f32[3,8,8,180]{3,2,1,0:T(8,128)}, u32[]{:S(2)}) copy-start(f32[3,8,8,180]{3,2,1,0:T(8,128)} %cx_in.1) | copy-start | bytes 414724
  2.1 0.9 %copy-start.2 = (f32[3,8,8,180]{3,2,1,0:T(8,128)S(1)}, f32[3,8,8,180]{3,2,1,0:T(8,128)}, u32[]{:S(2)}) copy-start(f32[3,8,8,180]{3,2,1,0:T(8,128)} %cy_in.1) | copy-start | bytes 414724
  3.1 0.7 %copy-start.3 = (s32[1152]{0:T(1024)S(1)}, s32[1152]{0:T(1024)}, u32[]{:S(2)}) copy-start(s32[1152]{0:T(1024)} %cut_in.1) | copy-start | bytes 13828
  3.8 0.7 %copy-start.4 = (s32[3,2]{0,1:T(2,128)S(1)}, s32[3,2]{0,1:T(2,128)}, u32[]{:S(2)}) copy-start(s32[3,2]{0,1:T(2,128)} %param.11) | copy-start | bytes 76
  4.4 0.7 copy-start.5

commit v6 on v5

--- a/solution.py
+++ b/solution.py
@@ -309,7 +309,7 @@
     back = (smooth_out, smooth_in, b_send, b_recv)
 
     def exchange(g, way):
-        for i in range(1, HALF):
+        for i in (4, 5, 3, 6, 2, 7, 1):
             seat_copy(g, i, *way).start()
         way[1][part(g, seat), :] = way[0][part(g, seat), :]
 

time: 68.5 us -> 67.8 us (0.990)
  no operation moved by 1% of the time
where the time goes in v6:
time: 67.8 us; the launch traced here: 67.3 us
  Pallas kernels  61.1 us (90%)
  local copies, waits for them, and re-layouts  5.08 us (7%)
  other arithmetic  1.09 us (2%)
    pallas_call x1, Pallas kernels, shards(): pl.pallas_call(step_kernel, out_shape=jax.ShapeDtypeStruct((F, S, NR, L,...  61.1 us
    unnamed x12, local copies, waits for them, and re-layouts  5.08 us

profile of v6, /device:TPU:1, one launch (start us, length us, event | category | flops | bytes accessed | tf_op | source)
XLA Modules:
  0.0 67.3 jit_solution(6574725984605125234)
XLA Ops:
  0.0 0.0 copy-start
  0.0 1.2 %copy-done = f32[5,3,8,8,180]{4,3,2,1,0:T(8,128)S(1)} copy-done((f32[5,3,8,8,180]{4,3,2,1,0:T(8,128)S(1)}, f32[5,3,8,8,180]{4,3,2,1,0:T(8,128)}, u32[]{:S(2)}) %copy-start) | copy-done | bytes 691224
  1.2 0.0 copy-start.1
  1.2 0.9 %copy-done.1 = f32[3,8,8,180]{3,2,1,0:T(8,128)S(1)} copy-done((f32[3,8,8,180]{3,2,1,0:T(8,128)S(1)}, f32[3,8,8,180]{3,2,1,0:T(8,128)}, u32[]{:S(2)}) %copy-start.1) | copy-done | bytes 138264
  2.1 0.0 copy-start.2
  2.1 0.9 %copy-done.2 = f32[3,8,8,180]{3,2,1,0:T(8,128)S(1)} copy-done((f32[3,8,8,180]{3,2,1,0:T(8,128)S(1)}, f32[3,8,8,180]{3,2,1,0:T(8,128)}, u32[]{:S(2)}) %copy-start.2) | copy-done | bytes 138264
  3.1 0.0 copy-start.3
  3.1 0.7 %copy-done.3 = s32[1152]{0:T(1024)S(1)} copy-done((s32[1152]{0:T(1024)S(1)}, s32[1152]{0:T(1024)}, u32[]{:S(2)}) %copy-start.3) | copy-done | bytes 4632
  3.8 0.0 copy-start.4
  3.8 0.7 %copy-done.4 = s32[3,2]{0,1:T(2,128)S(1)} copy-done((s32[3,2]{0,1:T(2,128)S(1)}, s32[3,2]{0,1:T(2,128)}, u32[]{:S(2)}) %copy-start.4) | copy-done | bytes 48
  4.4 0.0 copy-start.5
  4.4 0.7 copy-done.5
  5.1 61.1 %shard_map.73 = f32[5,3,8,8,180]{4,3,2,1,0:T(8,128)S(1)} custom-call(s32[3]{0:T(128)S(1)} %copy-done.5, s32[2,3]{1,0:T(2,128)S(1)} %bitcast.1, s32[1152]{0:T(1024)S(1)} %copy-done.3, f32[5,3,8,8,180]{4,3,2,1,0:T(8,128)S(1)} %copy-done, f32[3,8,8,180]{3,2,1,0:T(8,128)S(1)} %copy-done.1, f32[3,8,8,180]{3,2,1,0:T(8,128)S(1)} %copy-done.2, ...), custom_call_target="tpu_custom_call" | custom-call | tf_op jit(solution)/shard_map/pallas_call | solution.py:464
  66.2 1.1 %add.3 = f32[5,3,8,8,180]{4,3,2,1,0:T(8,128)} add(f32[5,3,8,8,180]{4,3,2,1,0:T(8,128)S(1)} %copy-done, f32[5,3,8,8,180]{4,3,2,1,0:T(8,128)S(1)} %shard_map.73) | non-fusion elementwise | flops 172800 | bytes 2073600 | tf_op jit(solution)/shard_map/add | solution.py:503
Async XLA Ops:
  0.0 1.2 %copy-start = (f32[5,3,8,8,180]{4,3,2,1,0:T(8,128)S(1)}, f32[5,3,8,8,180]{4,3,2,1,0:T(8,128)}, u32[]{:S(2)}) copy-start(f32[5,3,8,8,180]{4,3,2,1,0:T(8,128)} %state_in.1) | copy-start | bytes 2073604
  1.2 0.9 %copy-start.1 = (f32[3,8,8,180]{3,2,1,0:T(8,128)S(1)}, f32[3,8,8,180]{3,2,1,0:T(8,128)}, u32[]{:S(2)}) copy-start(f32[3,8,8,180]{3,2,1,0:T(8,128)} %cx_in.1) | copy-start | bytes 414724
  2.1 0.9 %copy-start.2 = (f32[3,8,8,180]{3,2,1,0:T(8,128)S(1)}, f32[3,8,8,180]{3,2,1,0:T(8,128)}, u32[]{:S(2)}) copy-start(f32[3,8,8,180]{3,2,1,0:T(8,128)} %cy_in.1) | copy-start | bytes 414724
  3.1 0.7 %copy-start.3 = (s32[1152]{0:T(1024)S(1)}, s32[1152]{0:T(1024)}, u32[]{:S(2)}) copy-start(s32[1152]{0:T(1024)} %cut_in.1) | copy-start | bytes 13828
  3.8 0.7 %copy-start.4 = (s32[3,2]{0,1:T(2,128)S(1)}, s32[3,2]{0,1:T(2,128)}, u32[]{:S(2)}) copy-start(s32[3,2]{0,1:T(2,128)} %param.11) | copy-start | bytes 76
  4.4 0.7 copy-start.5
